TPU v7x, 32 devices: a whole 2x2x4 slice. The times are simulated.
32 devices in a mesh: img: 16 (over z, y, core), seq: 2 (over x).
Axes of the slice: x: 2, y: 2, z: 4, core: 2. Of those that a mesh axis runs over, the one named last changes fastest.
Arguments:
- patches: bfloat16 [96, 2, 160, 768], P('img', 'seq'), may hold values from -6 to 6
- grid_shape: int32 [96, 2], P('img'), may hold values from 8 to 24, as said below
- split_rows: int32 [96], P('img'), may hold values from 1 to 11, as said below
- owner_shard: int32 [96], P('img'), may hold values from 0 to 1
- drop_masks: int32 [96, 2], P('img'), may hold values 0 or 1
- ln1_gain: float32 [768], replicated, may hold values from 0.25 to 1.75
- ln1_bias: float32 [768], replicated, may hold values from -3 to 3
- qkv_weight: bfloat16 [768, 2304], replicated, may hold values from -0.21875 to 0.21875
- qv_bias: float32 [1536], replicated, may hold values from -3 to 3
- proj_weight: bfloat16 [768, 768], replicated, may hold values from -0.875 to 0.875
- proj_bias: float32 [768], replicated, may hold values from -3 to 3
- ln2_gain: float32 [768], replicated, may hold values from 0.25 to 1.75
- ln2_bias: float32 [768], replicated, may hold values from -3 to 3
- fc1_weight: bfloat16 [768, 3072], replicated, may hold values from -0.21875 to 0.21875
- fc1_bias: float32 [3072], replicated, may hold values from -3 to 3
- fc2_weight: bfloat16 [3072, 768], replicated, may hold values from -0.21875 to 0.21875
- fc2_bias: float32 [768], replicated, may hold values from -3 to 3
- cotangent: bfloat16 [96, 2, 160, 768], P('img', 'seq'), may hold values from -6 to 6
Outputs:
- layer_out: bfloat16 [96, 2, 160, 768], P('img', 'seq')
- patches_grad: float32 [96, 2, 160, 768], P('img', 'seq')
- ln1_gain_grad: float32 [768], P(('img', 'seq'))
- ln1_bias_grad: float32 [768], P(('img', 'seq'))
- qkv_weight_grad: float32 [768, 2304], P(('img', 'seq'))
- qv_bias_grad: float32 [1536], P(('img', 'seq'))
- proj_weight_grad: float32 [768, 768], P(('img', 'seq'))
- proj_bias_grad: float32 [768], P(('img', 'seq'))
- ln2_gain_grad: float32 [768], P(('img', 'seq'))
- ln2_bias_grad: float32 [768], P(('img', 'seq'))
- fc1_weight_grad: float32 [768, 3072], P(('img', 'seq'))
- fc1_bias_grad: float32 [3072], P(('img', 'seq'))
- fc2_weight_grad: float32 [3072, 768], P(('img', 'seq'))
- fc2_bias_grad: float32 [768], P(('img', 'seq'))
Inputs may be any that keep to these rules, and one draw needn't show every extreme that they name: `grid_shape`: column 0 is the height, from 8 to 20; column 1 is the width, min(24, 280 // height), so an image has at most 280 patches. `split_rows`: both parts of every image hold at least one and at most 158 patches.
All inputs are finite; a program needn't handle non-finite values. No bound on the sum of `drop_masks` on one device may be relied on, other than what follows from the above.
Results may differ from a plain program's by a relative error of at most 0.014.
Values may be sent and summed in bfloat16 or wider, within the bound.
A program may use at most 192 MiB of HBM per device.

v0:
```python
import functools

import jax
import jax.numpy as jnp
from jax import lax
from jax.experimental import pallas as pl
from jax.experimental.pallas import tpu as pltpu
from jax.sharding import PartitionSpec as P

HEAD_DIM = 64
LN_EPS = 1e-06
KEEP_SCALE = 1.0 / 0.9
MASK_FILL = -1e30
BF16 = jnp.bfloat16
F32 = jnp.float32
MIB = 1024 * 1024


def dot_nn(a, b):
    return lax.dot_general(a, b, (((1,), (0,)), ((), ())), preferred_element_type=F32)


def dot_nt(a, b):
    return lax.dot_general(a, b, (((1,), (1,)), ((), ())), preferred_element_type=F32)


def dot_tn(a, b):
    return lax.dot_general(a, b, (((0,), (0,)), ((), ())), preferred_element_type=F32)


def norm_parts(values):
    row_mean = jnp.mean(values, axis=-1, keepdims=True)
    centred = values - row_mean
    variance = jnp.mean(centred * centred, axis=-1, keepdims=True)
    rstd = lax.rsqrt(variance + LN_EPS)
    return centred * rstd, rstd


def norm_back(d_normed, gain, unit, rstd):
    d_unit = d_normed * gain
    mean_one = jnp.mean(d_unit, axis=-1, keepdims=True)
    mean_two = jnp.mean(d_unit * unit, axis=-1, keepdims=True)
    return rstd * (d_unit - mean_one - unit * mean_two)


def gelu_both(values):
    cdf = 0.5 + 0.5 * lax.erf(values * 0.7071067811865476)
    return values * cdf, cdf + values * (0.3989422804014327 * jnp.exp(-0.5 * values * values))


class Facts:
    def __init__(self, refs, images, x):
        self.grid, self.split, self.owner, self.drop = refs
        self.images, self.x = images, x

    def __getitem__(self, key):
        image, k = key
        at = self.x * self.images + image
        if k >= 4:
            return self.drop[at, k - 4]
        if k % 2 == 1:
            own = (self.owner[at] == self.x).astype(jnp.int32)
            return own if k == 1 else 1 - own
        across = self.grid[at, 1]
        first = self.split[at] * across
        second = (self.grid[at, 0] - self.split[at]) * across
        return jnp.where(self.x == k // 2, first, second)


def row_valid(scal_ref, image, rows, half, axis):
    shape = (rows, 1) if axis == 0 else (1, rows)
    slot = lax.broadcasted_iota(jnp.int32, shape, axis)
    other = slot >= half
    place = jnp.where(other, slot - half, slot)
    count = jnp.where(other, scal_ref[image, 2], scal_ref[image, 0])
    special = jnp.where(other, scal_ref[image, 3], scal_ref[image, 1])
    return jnp.where(place < 2, special, (place - 2 < count).astype(jnp.int32)) > 0


def front_kernel(
    scal_ref, own_ref, oth_ref, g1_ref, b1_ref, wqkv_ref, qb_ref, vb_ref, wp_ref, pb_ref, g2_ref, b2_ref,
    n1_ref, qkv_ref, probs_ref, att_ref, mid_ref, n2_ref,
):
    image = pl.program_id(0)
    half, width = own_ref.shape[1], own_ref.shape[2]
    rows = 2 * half
    x = jnp.concatenate([own_ref[0].astype(F32), oth_ref[0].astype(F32)], axis=0)
    unit, _ = norm_parts(x)
    n1 = (unit * g1_ref[...] + b1_ref[...]).astype(BF16)
    n1_ref[0] = n1
    qkv_ref[0, :, :width] = ((dot_nn(n1, wqkv_ref[:, :width]) + qb_ref[...]).astype(BF16) * BF16(HEAD_DIM**-0.5))
    qkv_ref[0, :, width : 2 * width] = dot_nn(n1, wqkv_ref[:, width : 2 * width]).astype(BF16)
    qkv_ref[0, :, 2 * width :] = (dot_nn(n1, wqkv_ref[:, 2 * width :]) + vb_ref[...]).astype(BF16)
    fill = jnp.where(row_valid(scal_ref, image, rows, half, 0), 0.0, MASK_FILL)
    low_lane = lax.broadcasted_iota(jnp.int32, (rows, 128), 1) < HEAD_DIM
    for pair in range(width // 128):
        cut = slice(128 * pair, 128 * pair + 128)
        q2 = qkv_ref[0, :, cut]
        k2 = qkv_ref[0, :, width + 128 * pair : width + 128 * pair + 128]
        v2 = qkv_ref[0, :, 2 * width + 128 * pair : 2 * width + 128 * pair + 128]
        total = None
        for side in range(2):
            mine = low_lane if side == 0 else jnp.logical_not(low_lane)
            scores = dot_nt(k2, jnp.where(mine, q2, 0)) + fill
            top = jnp.max(scores, axis=0, keepdims=True)
            weight = jnp.exp(scores - top)
            probs = (weight * (1.0 / jnp.sum(weight, axis=0, keepdims=True))).astype(BF16)
            probs_ref[0, 2 * pair + side] = probs
            part = dot_tn(probs, jnp.where(mine, v2, 0))
            total = part if total is None else total + part
        att_ref[0, :, cut] = total.astype(BF16)
    keep = scal_ref[image, 4].astype(F32) * KEEP_SCALE
    branch = dot_nn(att_ref[0], wp_ref[...]) + pb_ref[...]
    middle = jnp.concatenate([own_ref[0].astype(F32), oth_ref[0].astype(F32)], axis=0) + keep * branch
    mid_ref[0] = middle
    unit, _ = norm_parts(middle)
    n2_ref[0] = (unit * g2_ref[...] + b2_ref[...]).astype(BF16)


def full(shape):
    zeros = (0,) * len(shape)
    return pl.BlockSpec(shape, lambda *_: zeros, pipeline_mode=pl.Buffered(1))


def front(scal, own, oth, w):
    images, half, width = own.shape
    rows = 2 * half
    heads = width // HEAD_DIM
    per = lambda *tail: pl.BlockSpec((1,) + tail, lambda i, s: (i,) + (0,) * len(tail))
    flops = 2 * images * rows * width * (4 * width + 4 * rows)
    return pl.pallas_call(
        front_kernel,
        grid_spec=pltpu.PrefetchScalarGridSpec(
            num_scalar_prefetch=1,
            grid=(images,),
            in_specs=[
                per(half, width), per(half, width), full((1, width)), full((1, width)),
                full((width, 3 * width)), full((1, width)), full((1, width)),
                full((width, width)), full((1, width)), full((1, width)), full((1, width)),
            ],
            out_specs=[
                per(rows, width), per(rows, 3 * width), per(heads, rows, rows),
                per(rows, width), per(rows, width), per(rows, width),
            ],
        ),
        out_shape=[
            jax.ShapeDtypeStruct((images, rows, width), BF16),
            jax.ShapeDtypeStruct((images, rows, 3 * width), BF16),
            jax.ShapeDtypeStruct((images, heads, rows, rows), BF16),
            jax.ShapeDtypeStruct((images, rows, width), BF16),
            jax.ShapeDtypeStruct((images, rows, width), F32),
            jax.ShapeDtypeStruct((images, rows, width), BF16),
        ],
        compiler_params=pltpu.CompilerParams(vmem_limit_bytes=56 * MIB),
        cost_estimate=pl.CostEstimate(flops=flops, transcendentals=images * heads * rows * rows, bytes_accessed=30_000_000),
        name="front",
    )(scal, own, oth, w["ln1_gain"], w["ln1_bias"], w["qkv_weight"], w["q_bias"], w["v_bias"],
      w["proj_weight"], w["proj_bias"], w["ln2_gain"], w["ln2_bias"])


def mlp_kernel(
    scal_ref, n2_ref, mid_ref, w1_ref, c1_ref, w2_ref, c2_ref,
    hid_ref, slope_ref, own_ref, oth_ref, acc_ref,
):
    step = pl.program_id(0)
    images, half, width = own_ref.shape
    rows = 2 * half
    hidden, slope = gelu_both(dot_nn(n2_ref[...], w1_ref[...]) + c1_ref[...])
    hidden = hidden.astype(BF16)
    hid_ref[...] = hidden
    slope_ref[...] = slope.astype(BF16)
    part = dot_nn(hidden, w2_ref[...])

    @pl.when(step == 0)
    def _():
        acc_ref[...] = part

    @pl.when(step > 0)
    def _():
        acc_ref[...] += part

    @pl.when(step == pl.num_programs(0) - 1)
    def _():
        for image in range(images):
            keep = scal_ref[image, 5].astype(F32) * KEEP_SCALE
            cut = slice(rows * image, rows * image + rows)
            final = mid_ref[cut, :] + keep * (acc_ref[cut, :] + c2_ref[...])
            out = jnp.where(row_valid(scal_ref, image, rows, half, 0), final, 0.0).astype(BF16)
            own_ref[image] = out[:half]
            oth_ref[image] = out[half:]


def mlp(scal, n2, middle, w, images, tile):
    tokens, width = n2.shape
    hidden_width = w["fc1_weight"].shape[1]
    half = tokens // images // 2
    return pl.pallas_call(
        mlp_kernel,
        grid_spec=pltpu.PrefetchScalarGridSpec(
            num_scalar_prefetch=1,
            grid=(hidden_width // tile,),
            in_specs=[
                full((tokens, width)), full((tokens, width)),
                pl.BlockSpec((width, tile), lambda j, s: (0, j)), pl.BlockSpec((1, tile), lambda j, s: (0, j)),
                pl.BlockSpec((tile, width), lambda j, s: (j, 0)), full((1, width)),
            ],
            out_specs=[
                pl.BlockSpec((tokens, tile), lambda j, s: (0, j)), pl.BlockSpec((tokens, tile), lambda j, s: (0, j)),
                full((images, half, width)), full((images, half, width)),
            ],
            scratch_shapes=[pltpu.VMEM((tokens, width), F32)],
        ),
        out_shape=[
            jax.ShapeDtypeStruct((tokens, hidden_width), BF16),
            jax.ShapeDtypeStruct((tokens, hidden_width), BF16),
            jax.ShapeDtypeStruct((images, half, width), BF16),
            jax.ShapeDtypeStruct((images, half, width), BF16),
        ],
        compiler_params=pltpu.CompilerParams(vmem_limit_bytes=56 * MIB),
        cost_estimate=pl.CostEstimate(flops=4 * tokens * width * hidden_width, transcendentals=2 * tokens * hidden_width, bytes_accessed=30_000_000),
        name="mlp",
    )(scal, n2, middle, w["fc1_weight"], w["fc1_bias"], w["fc2_weight"], w["fc2_bias"])


def put_rows(grad_ref, value, send_ref, keep_ref, mine, lead):
    grad_ref[...] = value
    run = 2 * send_ref.shape[-2]
    for k in range(grad_ref.shape[0] // (2 * run)):
        for ref, core in ((send_ref, 1 - mine), (keep_ref, mine)):
            for x in range(2):
                at = pl.multiple_of((2 * k + core) * run + x * (run // 2), 8)
                ref[lead + (k, x)] = grad_ref[pl.ds(at, run // 2), :].astype(BF16)


def put_folded(grad_ref, value, send_ref, keep_ref, mine):
    grad_ref[...] = value
    unit = send_ref.shape[-2] // 2
    side = grad_ref.shape[1] // 2
    for k in range(grad_ref.shape[0] // (4 * unit)):
        for ref, core in ((send_ref, 1 - mine), (keep_ref, mine)):
            for x in range(2):
                at = pl.multiple_of((4 * k + 2 * core + x) * unit, 8)
                piece = grad_ref[pl.ds(at, unit), :]
                ref[k, x] = jnp.concatenate([piece[:, :side], piece[:, side:]], axis=0).astype(BF16)


def mlp_back_kernel(
    scal_ref, mine_ref, own_ref, oth_ref, n2_ref, hid_ref, slope_ref, w1_ref, w2_ref,
    dn2_ref, s2_ref, k2_ref, s1_ref, k1_ref, c2_ref, c1_ref, dmlp_ref, grad_ref, acc_ref,
):
    step = pl.program_id(0)
    images, half, width = own_ref.shape
    rows = 2 * half
    mine = mine_ref[0]

    @pl.when(step == 0)
    def _():
        total = jnp.zeros((1, width), F32)
        for image in range(images):
            keep = scal_ref[image, 5].astype(F32) * KEEP_SCALE
            cot = jnp.concatenate([own_ref[image].astype(F32), oth_ref[image].astype(F32)], axis=0)
            live = row_valid(scal_ref, image, rows, half, 0)
            d_mlp = (jnp.where(live, cot, 0.0) * keep).astype(BF16)
            dmlp_ref[rows * image : rows * image + rows, :] = d_mlp
            total += jnp.sum(d_mlp.astype(F32), axis=0, keepdims=True)
        c2_ref[...] = total

    d_pre = slope_ref[...].astype(F32) * dot_nt(dmlp_ref[...], w2_ref[...])
    d_pre = d_pre.astype(BF16)
    c1_ref[...] = jnp.sum(d_pre.astype(F32), axis=0, keepdims=True)
    part = dot_nt(d_pre, w1_ref[...])
    put_folded(grad_ref, dot_tn(n2_ref[...], d_pre), s1_ref, k1_ref, mine)
    put_rows(grad_ref, dot_tn(hid_ref[...], dmlp_ref[...]), s2_ref, k2_ref, mine, (0,))

    @pl.when(step == 0)
    def _():
        acc_ref[...] = part

    @pl.when(step > 0)
    def _():
        acc_ref[...] += part

    @pl.when(step == pl.num_programs(0) - 1)
    def _():
        dn2_ref[...] = acc_ref[...]


def mlp_back(scal, mine, own, oth, n2, hidden, slope, w, unit1, unit2):
    tokens, width = n2.shape
    images, half, _ = own.shape
    hidden_width = hidden.shape[1]
    tile = width
    steps = hidden_width // tile
    runs1, runs2 = width // (4 * unit1), tile // (4 * unit2)
    col = pl.BlockSpec((tokens, tile), lambda j, s, m: (0, j))
    half1 = pl.BlockSpec((runs1, 2, 2 * unit1, tile // 2), lambda j, s, m: (0, 0, 0, j))
    half2 = pl.BlockSpec((1, runs2, 2, unit2, width), lambda j, s, m: (j, 0, 0, 0, 0))
    return pl.pallas_call(
        mlp_back_kernel,
        grid_spec=pltpu.PrefetchScalarGridSpec(
            num_scalar_prefetch=2,
            grid=(steps,),
            in_specs=[
                full((images, half, width)), full((images, half, width)), full((tokens, width)), col, col,
                pl.BlockSpec((width, tile), lambda j, s, m: (0, j)), pl.BlockSpec((tile, width), lambda j, s, m: (j, 0)),
            ],
            out_specs=[
                full((tokens, width)), half2, half2, half1, half1,
                full((1, width)), pl.BlockSpec((1, tile), lambda j, s, m: (0, j)),
            ],
            scratch_shapes=[
                pltpu.VMEM((tokens, width), BF16), pltpu.VMEM((width, width), F32), pltpu.VMEM((tokens, width), F32),
            ],
        ),
        out_shape=[
            jax.ShapeDtypeStruct((tokens, width), F32),
            jax.ShapeDtypeStruct((steps, runs2, 2, unit2, width), BF16),
            jax.ShapeDtypeStruct((steps, runs2, 2, unit2, width), BF16),
            jax.ShapeDtypeStruct((runs1, 2, 2 * unit1, hidden_width // 2), BF16),
            jax.ShapeDtypeStruct((runs1, 2, 2 * unit1, hidden_width // 2), BF16),
            jax.ShapeDtypeStruct((1, width), F32),
            jax.ShapeDtypeStruct((1, hidden_width), F32),
        ],
        compiler_params=pltpu.CompilerParams(vmem_limit_bytes=58 * MIB),
        cost_estimate=pl.CostEstimate(flops=8 * tokens * width * hidden_width, transcendentals=0, bytes_accessed=35_000_000),
        name="mlp_back",
    )(scal, mine, own, oth, n2, hidden, slope, w["fc1_weight"], w["fc2_weight"])


def attend_back_kernel(
    scal_ref, own_ref, oth_ref, dn2_ref, mid_ref, qkv_ref, probs_ref, wp_ref, g2_ref,
    dmid_ref, dbr_ref, djoin_ref, g2g_ref, g2b_ref, pbg_ref, qbg_ref, vbg_ref, datt_ref,
):
    image = pl.program_id(0)
    half, width = own_ref.shape[1], own_ref.shape[2]
    rows = 2 * half
    live = row_valid(scal_ref, image, rows, half, 0)
    d_final = jnp.where(live, jnp.concatenate([own_ref[0].astype(F32), oth_ref[0].astype(F32)], axis=0), 0.0)
    unit, rstd = norm_parts(mid_ref[0])
    dn2 = dn2_ref[0]
    gain_part = jnp.sum(dn2 * unit, axis=0, keepdims=True)
    bias_part = jnp.sum(dn2, axis=0, keepdims=True)
    d_middle = d_final + norm_back(dn2, g2_ref[...], unit, rstd)
    dmid_ref[0] = d_middle
    keep = scal_ref[image, 4].astype(F32) * KEEP_SCALE
    d_branch = (d_middle * keep).astype(BF16)
    dbr_ref[0] = d_branch
    proj_part = jnp.sum(d_branch.astype(F32), axis=0, keepdims=True)
    datt_ref[...] = dot_nt(d_branch, wp_ref[...]).astype(BF16)
    low_lane = lax.broadcasted_iota(jnp.int32, (rows, 128), 1) < HEAD_DIM
    for pair in range(width // 128):
        cut = slice(128 * pair, 128 * pair + 128)
        q2 = qkv_ref[0, :, cut]
        k2 = qkv_ref[0, :, width + 128 * pair : width + 128 * pair + 128]
        v2 = qkv_ref[0, :, 2 * width + 128 * pair : 2 * width + 128 * pair + 128]
        a2 = datt_ref[:, cut]
        dq = dk = dv = None
        for side in range(2):
            mine = low_lane if side == 0 else jnp.logical_not(low_lane)
            probs_low = probs_ref[0, 2 * pair + side]
            probs = probs_low.astype(F32)
            a_side = jnp.where(mine, a2, 0)
            d_probs = dot_nt(v2, a_side)
            inner = jnp.sum(probs * d_probs, axis=0, keepdims=True)
            d_scores = (probs * (d_probs - inner)).astype(BF16)
            dq_part = dot_tn(d_scores, jnp.where(mine, k2, 0))
            dk_part = dot_nn(d_scores, jnp.where(mine, q2, 0))
            dv_part = dot_nn(probs_low, a_side)
            dq = dq_part if dq is None else dq + dq_part
            dk = dk_part if dk is None else dk + dk_part
            dv = dv_part if dv is None else dv + dv_part
        djoin_ref[0, :, cut] = (dq * HEAD_DIM**-0.5).astype(BF16)
        djoin_ref[0, :, width + 128 * pair : width + 128 * pair + 128] = dk.astype(BF16)
        djoin_ref[0, :, 2 * width + 128 * pair : 2 * width + 128 * pair + 128] = dv.astype(BF16)
    q_part = jnp.sum(djoin_ref[0, :, :width].astype(F32), axis=0, keepdims=True)
    v_part = jnp.sum(djoin_ref[0, :, 2 * width :].astype(F32), axis=0, keepdims=True)
    sums = ((g2g_ref, gain_part), (g2b_ref, bias_part), (pbg_ref, proj_part), (qbg_ref, q_part), (vbg_ref, v_part))

    @pl.when(image == 0)
    def _():
        for ref, part in sums:
            ref[...] = part

    @pl.when(image > 0)
    def _():
        for ref, part in sums:
            ref[...] += part


def attend_back(scal, own, oth, dn2, middle, qkv, probs, w):
    images, half, width = own.shape
    rows = 2 * half
    heads = width // HEAD_DIM
    per = lambda *tail: pl.BlockSpec((1,) + tail, lambda i, s: (i,) + (0,) * len(tail))
    vec = jax.ShapeDtypeStruct((1, width), F32)
    return pl.pallas_call(
        attend_back_kernel,
        grid_spec=pltpu.PrefetchScalarGridSpec(
            num_scalar_prefetch=1,
            grid=(images,),
            in_specs=[
                per(half, width), per(half, width), per(rows, width), per(rows, width), per(rows, 3 * width),
                per(heads, rows, rows), full((width, width)), full((1, width)),
            ],
            out_specs=[per(rows, width), per(rows, width), per(rows, 3 * width)] + [full((1, width))] * 5,
            scratch_shapes=[pltpu.VMEM((rows, width), BF16)],
        ),
        out_shape=[
            jax.ShapeDtypeStruct((images, rows, width), F32),
            jax.ShapeDtypeStruct((images, rows, width), BF16),
            jax.ShapeDtypeStruct((images, rows, 3 * width), BF16),
            vec, vec, vec, vec, vec,
        ],
        compiler_params=pltpu.CompilerParams(vmem_limit_bytes=56 * MIB),
        cost_estimate=pl.CostEstimate(flops=2 * images * rows * width * (width + 8 * rows), transcendentals=0, bytes_accessed=35_000_000),
        name="attend_back",
    )(scal, own, oth, dn2, middle, qkv, probs, w["proj_weight"], w["ln2_gain"])


def tail_kernel(
    mine_ref, n1_ref, djoin_ref, att_ref, dbr_ref, wqkv_ref, xo_ref, xt_ref, dmid_ref, g1_ref,
    send_ref, keep_ref, go_ref, gt_ref, g1g_ref, g1b_ref, grad_ref, acc_ref,
):
    step = pl.program_id(0)
    last = pl.num_programs(0) - 1
    images, half, width = xo_ref.shape
    rows = 2 * half
    mine = mine_ref[0]

    @pl.when(step < last)
    def _():
        put_folded(grad_ref, dot_tn(n1_ref[...], djoin_ref[...]), send_ref, keep_ref, mine)
        part = dot_nt(djoin_ref[...], wqkv_ref[...])

        @pl.when(step == 0)
        def _():
            acc_ref[...] = part

        @pl.when(step > 0)
        def _():
            acc_ref[...] += part

    @pl.when(step == last)
    def _():
        put_folded(grad_ref, dot_tn(att_ref[...], dbr_ref[...]), send_ref, keep_ref, mine)
        gain_sum = jnp.zeros((1, width), F32)
        bias_sum = jnp.zeros((1, width), F32)
        for image in range(images):
            x = jnp.concatenate([xo_ref[image].astype(F32), xt_ref[image].astype(F32)], axis=0)
            unit, rstd = norm_parts(x)
            dn1 = acc_ref[rows * image : rows * image + rows, :]
            gain_sum += jnp.sum(dn1 * unit, axis=0, keepdims=True)
            bias_sum += jnp.sum(dn1, axis=0, keepdims=True)
            out = dmid_ref[rows * image : rows * image + rows, :] + norm_back(dn1, g1_ref[...], unit, rstd)
            go_ref[image] = out[:half]
            gt_ref[image] = out[half:].astype(BF16)
        g1g_ref[...] = gain_sum
        g1b_ref[...] = bias_sum


def tail(mine, n1, d_join, attended, d_branch, own, oth, d_middle, w, unit):
    tokens, width = n1.shape
    images, half, _ = own.shape
    runs = width // (4 * unit)
    halves = pl.BlockSpec((runs, 2, 2 * unit, width // 2), lambda j, m: (0, 0, 0, j))
    clip = lambda j: jnp.minimum(j, 2)
    return pl.pallas_call(
        tail_kernel,
        grid_spec=pltpu.PrefetchScalarGridSpec(
            num_scalar_prefetch=1,
            grid=(4,),
            in_specs=[
                full((tokens, width)), pl.BlockSpec((tokens, width), lambda j, m: (0, clip(j))), full((tokens, width)),
                full((tokens, width)), pl.BlockSpec((width, width), lambda j, m: (0, clip(j))),
                full((images, half, width)), full((images, half, width)), full((tokens, width)), full((1, width)),
            ],
            out_specs=[
                halves, halves, full((images, half, width)), full((images, half, width)),
                full((1, width)), full((1, width)),
            ],
            scratch_shapes=[pltpu.VMEM((width, width), F32), pltpu.VMEM((tokens, width), F32)],
        ),
        out_shape=[
            jax.ShapeDtypeStruct((runs, 2, 2 * unit, 2 * width), BF16),
            jax.ShapeDtypeStruct((runs, 2, 2 * unit, 2 * width), BF16),
            jax.ShapeDtypeStruct((images, half, width), F32),
            jax.ShapeDtypeStruct((images, half, width), BF16),
            jax.ShapeDtypeStruct((1, width), F32),
            jax.ShapeDtypeStruct((1, width), F32),
        ],
        compiler_params=pltpu.CompilerParams(vmem_limit_bytes=56 * MIB),
        cost_estimate=pl.CostEstimate(flops=14 * tokens * width * width, transcendentals=0, bytes_accessed=35_000_000),
        name="tail",
    )(mine, n1, d_join, attended, d_branch, w["qkv_weight"], own, oth, d_middle, w["ln1_gain"])


def open_kernel(
    grid_ref, split_ref, owner_ref, drop_ref, patches_ref, cot_ref, g1_ref, b1_ref, qv_ref, pb_ref, g2_ref, b2_ref, c1_ref, c2_ref, wqkv_hbm, wp_hbm,
    unit_ref, rstd_ref, qkv_ref, probs_ref, att_ref, mid_ref, n2_ref, rows_ref, cot_oth,
    xbuf, wqkv_ref, wp_ref, load_sem, send_sem, recv_sem,
):
    image = pl.program_id(0)
    images, rows, width = xbuf.shape
    half = rows // 2
    line = lax.axis_index("img")
    x_at = lax.axis_index("seq")
    across = (line, 1 - x_at)
    scal_ref = Facts((grid_ref, split_ref, owner_ref, drop_ref), images, x_at)
    loads = [
        pltpu.make_async_copy(wqkv_hbm, wqkv_ref, load_sem.at[0]),
        pltpu.make_async_copy(wp_hbm, wp_ref, load_sem.at[1]),
    ]

    def own_copy(i):
        return pltpu.make_async_copy(patches_ref.at[x_at * images + i], xbuf.at[i, pl.ds(0, half)], load_sem.at[2 + i])

    def far_copy(i):
        return pltpu.make_async_remote_copy(
            src_ref=patches_ref.at[(1 - x_at) * images + i], dst_ref=xbuf.at[i, pl.ds(half, half)],
            send_sem=send_sem.at[i], recv_sem=recv_sem.at[i], device_id=across, device_id_type=MESH,
        )

    def cot_copy():
        return pltpu.make_async_remote_copy(
            src_ref=cot_ref.at[pl.ds((1 - x_at) * images, images)], dst_ref=cot_oth,
            send_sem=send_sem.at[images], recv_sem=recv_sem.at[images], device_id=across, device_id_type=MESH,
        )

    @pl.when(image == 0)
    def _():
        barrier = pltpu.get_barrier_semaphore()
        pl.semaphore_signal(barrier, inc=1, device_id=across, device_id_type=MESH)
        own_copy(0).start()
        loads[0].start()
        pl.semaphore_wait(barrier, 1)
        for i in range(images):
            far_copy(i).start()
        for i in range(1, images):
            own_copy(i).start()
        loads[1].start()
        row = lambda ref: ref[...].reshape(1, -1)
        rows_ref[...] = jnp.zeros_like(rows_ref)
        for k in range(c1_ref.shape[0] // width):
            rows_ref[k : k + 1, :] = row(c1_ref)[:, k * width : k * width + width]
        for k, ref in enumerate((c2_ref, g1_ref, b1_ref, g2_ref, b2_ref, pb_ref)):
            rows_ref[4 + k : 5 + k, :] = row(ref)
        rows_ref[10:11, :] = row(qv_ref)[:, :width]
        rows_ref[11:12, :] = row(qv_ref)[:, width:]
        loads[0].wait()
        loads[1].wait()

    for i in range(images):

        @pl.when(image == i)
        def _():
            own_copy(i).wait()
            far_copy(i).wait()

    @pl.when(image == 1)
    def _():
        cot_copy().start()

    vector = lambda k: rows_ref[k : k + 1, :]
    unit, rstd = norm_parts(xbuf[image].astype(F32))
    unit_ref[0] = unit.astype(BF16)
    rstd_ref[0] = rstd
    n1 = (unit * vector(5) + vector(6)).astype(BF16)
    qkv_ref[0, :, :width] = ((dot_nn(n1, wqkv_ref[:, :width]) + vector(10)).astype(BF16) * BF16(HEAD_DIM**-0.5))
    qkv_ref[0, :, width : 2 * width] = dot_nn(n1, wqkv_ref[:, width : 2 * width]).astype(BF16)
    qkv_ref[0, :, 2 * width :] = (dot_nn(n1, wqkv_ref[:, 2 * width :]) + vector(11)).astype(BF16)
    fill = jnp.where(row_valid(scal_ref, image, rows, half, 0), 0.0, MASK_FILL)
    low_lane = lax.broadcasted_iota(jnp.int32, (rows, 128), 1) < HEAD_DIM
    for pair in range(width // 128):
        cut, k_cut, v_cut = (slice(k * width + 128 * pair, k * width + 128 * pair + 128) for k in range(3))
        q2, k2, v2 = qkv_ref[0, :, cut], qkv_ref[0, :, k_cut], qkv_ref[0, :, v_cut]
        total = None
        for side in range(2):
            mine = low_lane if side == 0 else jnp.logical_not(low_lane)
            scores = dot_nt(k2, jnp.where(mine, q2, 0)) + fill
            top = jnp.max(scores, axis=0, keepdims=True)
            weight = jnp.exp(scores - top)
            probs = (weight * (1.0 / jnp.sum(weight, axis=0, keepdims=True))).astype(BF16)
            probs_ref[0, 2 * pair + side] = probs
            part = dot_tn(probs, jnp.where(mine, v2, 0))
            total = part if total is None else total + part
        att_ref[0, :, cut] = total.astype(BF16)
    keep = scal_ref[image, 4].astype(F32) * KEEP_SCALE
    middle = xbuf[image].astype(F32) + keep * (dot_nn(att_ref[0], wp_ref[...]) + vector(9))
    mid_ref[0] = middle
    unit, _ = norm_parts(middle)
    n2_ref[0] = (unit * vector(7) + vector(8)).astype(BF16)

    @pl.when(image == images - 1)
    def _():
        cot_copy().wait()


def opening(facts, patches, cotangent, args):
    all_images, half, width = patches.shape
    images = all_images // 2
    rows = 2 * half
    heads = width // HEAD_DIM
    per = lambda *tail: pl.BlockSpec((1,) + tail, lambda i: (i,) + (0,) * len(tail))
    hbm = pl.BlockSpec(memory_space=pl.ANY)
    vmem = pl.BlockSpec(memory_space=pltpu.VMEM)
    dma = pltpu.SemaphoreType.DMA
    shape = jax.ShapeDtypeStruct
    return pl.pallas_call(
        open_kernel,
        grid=(images,),
        in_specs=[pl.BlockSpec(memory_space=pltpu.SMEM)] * 4 + [hbm, hbm] + [vmem] * 8 + [hbm, hbm],
        out_specs=[
            per(rows, width), per(rows, 1), per(rows, 3 * width), per(heads, rows, rows), per(rows, width),
            per(rows, width), per(rows, width), vmem, hbm,
        ],
        out_shape=[
            shape((images, rows, width), BF16), shape((images, rows, 1), F32), shape((images, rows, 3 * width), BF16),
            shape((images, heads, rows, rows), BF16), shape((images, rows, width), BF16), shape((images, rows, width), F32),
            shape((images, rows, width), BF16), shape((16, width), F32), shape((images, half, width), BF16),
        ],
        scratch_shapes=[
            pltpu.VMEM((images, rows, width), BF16), pltpu.VMEM((width, 3 * width), BF16), pltpu.VMEM((width, width), BF16),
            dma((2 + images,)), dma((images + 1,)), dma((images + 1,)),
        ],
        compiler_params=pltpu.CompilerParams(collective_id=1, has_side_effects=True, vmem_limit_bytes=63 * MIB),
        name="opening",
    )(*facts, patches, cotangent, *args)


def emit_kernel(
    fc2_ref, fc1_ref, u_ref, proj_ref, sums_ref, rows_ref, w_ref, own_ref, back_ref, lo_ref,
    out_ref, grad_ref, l1g, l1b, qkvg, qvb, projg, pjb, l2g, l2b, fc1g, f1b, fc2g, f2b, buf, own_buf, back_buf, lo_buf, sems,
):
    side = lax.axis_index("seq")
    owner = 2 * lax.axis_index("img") + side
    images, half, width = own_ref.shape
    unit = u_ref.shape[0]
    arrivals = [
        pltpu.make_async_copy(back_ref, back_buf, sems.at[0]), pltpu.make_async_copy(own_ref, own_buf, sems.at[1]),
        pltpu.make_async_copy(lo_ref, lo_buf, sems.at[2]),
    ]
    for copy in arrivals:
        copy.start()
    arrivals[0].wait()
    buf[...] = back_buf[...].astype(F32)
    other = pltpu.make_async_copy(buf, grad_ref.at[pl.ds((1 - side) * images, images)], sems.at[0])
    other.start()
    arrivals[1].wait()
    mine = pltpu.make_async_copy(own_buf, grad_ref.at[pl.ds(side * images, images)], sems.at[1])
    mine.start()
    arrivals[2].wait()
    keep = pltpu.make_async_copy(lo_buf, out_ref, sems.at[2])
    keep.start()
    fc2g[...] = fc2_ref[...]
    fc1g[...] = fc1_ref[...]
    projg[...] = proj_ref[...]
    lane = lax.broadcasted_iota(jnp.int32, (unit, width), 1)
    slot = lax.broadcasted_iota(jnp.int32, (unit, width), 0)
    here = lane == owner * unit + slot
    column = lambda k: jnp.sum(jnp.where(here, rows_ref[k : k + 1, :], 0.0), axis=1, keepdims=True)
    gain, bias = column(5), column(6)
    gain_sum = bias_sum = 0.0
    for k, at in enumerate((2, 0, 3)):
        cut = slice(k * width, k * width + width)
        total, weight, sums = u_ref[:, cut], w_ref[:, cut].astype(F32), sums_ref[at : at + 1, :]
        qkvg[:, cut] = gain * total + bias * sums
        gain_sum += jnp.sum(weight * total, axis=1, keepdims=True)
        bias_sum += jnp.sum(weight * sums, axis=1, keepdims=True)
    diag = lax.broadcasted_iota(jnp.int32, (unit, 128), 1) == lax.broadcasted_iota(jnp.int32, (unit, 128), 0)
    for ref, value in ((l1g, gain_sum), (l1b, bias_sum)):
        ref[...] = jnp.sum(jnp.where(diag, value, 0.0), axis=0, keepdims=True)[0, :unit]
    for ref, at, count in ((pjb, 4, 1), (l2g, 5, 1), (l2b, 6, 1), (f2b, 11, 1), (f1b, 7, 4), (qvb, 2, 2)):
        size = unit * count
        place = owner * size
        which, start = place // width, place % width
        row = sums_ref[at : at + 1, :]
        for k in range(1, count):
            row = jnp.where(which == k, sums_ref[at + k : at + k + 1, :], row)
        sel = lax.broadcasted_iota(jnp.int32, (size, width), 1) == start + lax.broadcasted_iota(jnp.int32, (size, width), 0)
        tall = jnp.sum(jnp.where(sel, row, 0.0), axis=1, keepdims=True)
        eye = lax.broadcasted_iota(jnp.int32, (size, 128), 1) == lax.broadcasted_iota(jnp.int32, (size, 128), 0)
        ref[...] = jnp.sum(jnp.where(eye, tall, 0.0), axis=0, keepdims=True)[0, :size]
    keep.wait()
    mine.wait()
    other.wait()


def emit(fc2, fc1, u, proj, sums, rows, qkv_weight, own, back, layer_out):
    images, half, width = own.shape
    unit = u.shape[0]
    hbm = pl.BlockSpec(memory_space=pl.ANY)
    whole = lambda v: pl.BlockSpec(v.shape, lambda i: (0,) * len(v.shape))
    shape = lambda *dims: jax.ShapeDtypeStruct(dims, F32)
    outs = [
        shape(unit), shape(unit), shape(unit, 3 * width), shape(2 * unit), shape(unit, width), shape(unit), shape(unit),
        shape(unit), shape(*fc1.shape), shape(fc1.shape[1] // GROUP), shape(*fc2.shape), shape(unit),
    ]
    return pl.pallas_call(
        emit_kernel,
        grid=(1,),
        in_specs=[whole(v) for v in (fc2, fc1, u, proj, sums, rows)]
        + [pl.BlockSpec((unit, 3 * width), lambda i: (2 * lax.axis_index("img") + lax.axis_index("seq"), 0)), hbm, hbm, hbm],
        out_specs=[hbm, hbm] + [whole(v) for v in outs],
        scratch_shapes=[
            pltpu.VMEM(own.shape, F32), pltpu.VMEM(own.shape, F32), pltpu.VMEM(back.shape, BF16),
            pltpu.VMEM(layer_out.shape, BF16), pltpu.SemaphoreType.DMA((3,)),
        ],
        out_shape=[jax.ShapeDtypeStruct(layer_out.shape, BF16), shape(2 * images, half, width)] + outs,
        compiler_params=pltpu.CompilerParams(vmem_limit_bytes=63 * MIB),
        name="emit",
    )(fc2, fc1, u, proj, sums, rows, qkv_weight, own, back, layer_out)


MESH = pl.DeviceIdType.MESH
PARTS = 7
SLOTS = 3
GROUP = 32


class Far:
    def __init__(self, ends, send_sem, recv_sem, peer):
        self.parts = (ends, send_sem, recv_sem, peer)
        self.build().start()

    def build(self):
        ends, send_sem, recv_sem, peer = self.parts
        src, dst = ends()
        return pltpu.make_async_remote_copy(
            src_ref=src, dst_ref=dst, send_sem=send_sem(), recv_sem=recv_sem(), device_id=peer, device_id_type=MESH
        )

    def wait(self):
        self.build().wait()


class Parcel:
    def __init__(self, keep, send, landing, levels, sems, order, place, names="wvyx"):
        self.keep, self.send, self.landing, self.levels, self.sems = keep, send, landing, levels, sems
        self.order, self.place, self.names = order, place, names

    def copy(self, src, dst, slot, peer):
        send_sem, recv_sem = self.sems
        return pltpu.make_async_remote_copy(
            src_ref=src, dst_ref=dst, send_sem=send_sem(slot), recv_sem=recv_sem(slot), device_id=peer, device_id_type=MESH
        )

    def bring(self, step):
        if step == 0:
            return self.copy(self.send(), self.landing(), 0, self.place["core"][1])
        name, used = self.order[step - 1], self.order[:step]
        spot = tuple(
            self.place[n][2] if n == name else self.place[n][0] if n in used else slice(None) for n in self.names
        )
        return self.copy(self.keep().at[spot], self.levels(step - 1), step, self.place[name][1])

    def start(self):
        self.bring(0).start()

    def gather(self, step):
        self.bring(step).wait()
        return self.add(step)

    def add(self, step):
        used = self.order[:step]
        left = [n for n in self.names if n not in used]
        arrived = self.levels(step - 1) if step else self.landing()

        def one(i):
            at = {}
            for n in reversed(left):
                at[n] = i % 2
                i = i // 2
            inner = tuple(at[n] for n in left)
            spot = tuple(at[n] if n in at else self.place[n][0] for n in self.names)
            total = self.keep()[spot].astype(F32) + arrived[inner].astype(F32)
            if step == len(self.order):
                return total
            self.keep()[spot] = total.astype(BF16)

        if not left:
            return one(0)
        pl.loop(0, 2 ** len(left))(lambda i: one(i) and None)

    def launch(self, step):
        self.bring(step + 1).start()

    def move(self, step):
        self.gather(step)
        self.launch(step)


class HalfParcel(Parcel):
    def launch(self, step):
        if step < 3:
            return super().launch(step)

        @pl.when(self.goes)
        def _():
            self.bring(4).start()

    def finish(self, write):
        @pl.when(self.goes)
        def _():
            self.bring(4).wait_send()

        @pl.when(self.mine)
        def _():
            self.bring(4).wait_recv()
            write(self.add(4))


def level_shapes(names, order, rows, cols):
    return [
        (2,) * len([n for n in names if n not in order[: step + 1]]) + (rows, cols) for step in range(len(order))
    ]


ORDERS = ("yvxw", "vxyw", "xwyv", "yxwv", "vwyx", "yvxw", "vywx")
FC2_A, FC2_B, FC1_A, FC1_B, VAL_PROJ, QUERY, KEY = range(7)


def rest_kernel(
    grid_ref, split_ref, owner_ref, drop_ref, cot_hbm, cot_oth, n2_hbm, mid_hbm, qkv_hbm, probs_hbm, w1_hbm, w2_hbm, wp_hbm, wqkv_hbm, unit_hbm, rstd_hbm,
    att_hbm, rows_ref,
    fc2_ref, fc1_ref, qkvg_ref, projg_ref, vec_ref, out_ref, grad_ref, back_ref,
    cot, rstd_one, dn2, mid, acc, left, right, wbuf, qkv, probs, djoin, datt, tile, ost, gsend, grecv, vec, vget,
    keep_a, send_a, land_a, keep_b, send_b, land_b, keep_c, send_c, land_c, *others,
):
    levels = [others[4 * k : 4 * k + 4] for k in range(PARTS)]
    (load_sem, probs_sem, qkv_sem, w_sem, send_sem, recv_sem, side_send, side_recv, vec_send, vec_recv, out_sem,
     free_sem) = others[4 * PARTS :]
    images, rows, width = dn2.shape
    half = rows // 2
    pairs = width // 128
    steps = w1_hbm.shape[1] // width
    line = lax.axis_index("img")
    x = lax.axis_index("seq")
    core = line % 2
    y = (line // 2) % 2
    z = line // 4
    sibling = (line + 1 - 2 * core, x)
    level = (line + 2 - 4 * y, x)
    across = (line, 1 - x)
    scal_ref = Facts((grid_ref, split_ref, owner_ref, drop_ref), images, x)
    zv, zw = z % 2, z // 2
    near_z = (line + 4 - 8 * zv, x)
    far_z = (line + 8 - 16 * zw, x)
    peers = [sibling, level, across, near_z, far_z]
    barrier = pltpu.get_barrier_semaphore()
    for peer in peers:
        pl.semaphore_signal(barrier, inc=1, device_id=peer, device_id_type=MESH)

    loads = []

    def fetch(src, dst):
        copy = pltpu.make_async_copy(src, dst, load_sem.at[len(loads)])
        copy.start()
        loads.append(copy)
        return copy

    def probs_copy(index, slot):
        return pltpu.make_async_copy(
            probs_hbm.at[index // pairs, pl.ds(2 * (index % pairs), 2)], probs.at[slot], probs_sem.at[slot]
        )

    def qkv_copy(i, slot):
        return pltpu.make_async_copy(qkv_hbm.at[i], qkv.at[slot], qkv_sem.at[slot])

    def w1_copy(t, slot):
        at = pl.multiple_of(t * width, 128)
        return pltpu.make_async_copy(w1_hbm.at[:, pl.ds(at, width)], wbuf.at[slot], w_sem.at[slot])

    def w2_copy(t, slot):
        at = pl.multiple_of(t * width, 128)
        return pltpu.make_async_copy(w2_hbm.at[pl.ds(at, width), :], wbuf.at[2 + slot], w_sem.at[2 + slot])

    first = [fetch(cot_hbm.at[pl.ds(x * images, images)], cot.at[:, pl.ds(0, half)]), fetch(cot_oth, cot.at[:, pl.ds(half, half)]), fetch(n2_hbm, left)]
    w1_copy(0, 0).start()
    w2_copy(0, 0).start()
    mid_in = fetch(mid_hbm, mid)
    for slot in range(SLOTS):
        probs_copy(slot, slot).start()
    for slot in range(2):
        qkv_copy(slot, slot).start()

    place = {
        "core": (core, sibling), "y": (y, level, 1 - y), "x": (x, across, 1 - x),
        "v": (zv, near_z, 1 - zv), "w": (zw, far_z, 1 - zw),
    }
    homes = [
        (keep_a.at[0], send_a, land_a), (keep_a.at[1], send_a, land_a),
        (keep_b.at[0], send_b.at[0], land_b.at[0]), (keep_b.at[1], send_b.at[1], land_b.at[1]),
        (keep_b.at[2], send_b.at[0], land_b.at[0]),
        (keep_c.at[0], send_c.at[0], land_c.at[0]), (keep_c.at[1], send_c.at[1], land_c.at[1]),
    ]
    parcels = []
    for k in range(PARTS):
        keep, send, land = (lambda k=k, n=n: homes[k][n] for n in range(3))
        sems = (lambda slot, k=k: send_sem.at[k, slot]), (lambda slot, k=k: recv_sem.at[k, slot])
        build = HalfParcel if k < 2 else Parcel
        parcels.append(
            build(keep, send, land, lambda step, k=k: levels[k][step], sems, ORDERS[k], place, "vyx" if k < 2 else "wvyx")
        )
    for k in range(2):
        parcels[k].goes, parcels[k].mine = zw != k, zw == k
    free_slot = {FC2_A: 0, FC1_A: 1}
    needs = {FC2_B: 0, VAL_PROJ: 1}

    def release(k):
        pl.semaphore_signal(free_sem.at[free_slot[k]], inc=1, device_id=sibling, device_id_type=MESH)

    def start(k):
        if k in needs:
            pl.semaphore_wait(free_sem.at[needs[k]], 1)
        parcels[k].start()

    r, c = keep_b.shape[-2], keep_b.shape[-1]
    unit, side_cols = r // 2, c // 2

    def put_block_rows(k, zz):
        for ref, who in ((send_a, 1 - core), (keep_a.at[k], core)):
            for b in range(2):
                for e in range(2):
                    at = pl.multiple_of((2 * b + who) * 4 * r + e * 2 * r, 8)
                    ref[zz, b, e] = tile[pl.ds(at, 2 * r), :].astype(BF16)

    def put_folds(send, kept, t):
        spot = pl.ds(pl.multiple_of(t * side_cols, 128), side_cols)

        @pl.loop(0, 8)
        def _(k):
            for ref, who in ((send, 1 - core), (kept, core)):
                for e in range(2):
                    at = pl.multiple_of((4 * k + 2 * who + e) * unit, 8)
                    piece = tile[pl.ds(at, unit), :]
                    ref[k // 4, (k // 2) % 2, k % 2, e, :, spot] = jnp.concatenate(
                        [piece[:, :side_cols], piece[:, side_cols:]], axis=0
                    ).astype(BF16)

    def step_one(k):
        parcels[k].gather(0)
        if k in free_slot:
            release(k)
        parcels[k].launch(0)

    flat = lambda ref: ref[...].reshape(images * rows, ref.shape[-1])
    column = lambda k: djoin[:, :, k * width : k * width + width].reshape(images * rows, width)

    vec[...] = jnp.zeros_like(vec)
    acc[...] = jnp.zeros_like(acc)
    dn2[...] = jnp.zeros_like(dn2)
    for copy in first:
        copy.wait()
    for i in range(images):
        gate = scal_ref[i, 5].astype(F32) * KEEP_SCALE
        live = row_valid(scal_ref, i, rows, half, 0)
        d_mlp = (jnp.where(live, cot[i].astype(F32), 0.0) * gate).astype(BF16)
        right[i] = d_mlp
        vec[11:12, :] += jnp.sum(d_mlp.astype(F32), axis=0, keepdims=True)
    pl.semaphore_wait(barrier, len(peers))

    wp_copy = pltpu.make_async_copy(wp_hbm, wbuf.at[2], w_sem.at[2])

    def wqkv_copy(k, slot):
        return pltpu.make_async_copy(wqkv_hbm.at[:, pl.ds(k * width, width)], wbuf.at[slot], w_sem.at[slot])

    @pl.loop(0, steps)
    def _(t):
        slot = t % 2
        w1_copy(t, slot).wait()
        w2_copy(t, slot).wait()

        @pl.when(t + 1 < steps)
        def _():
            w1_copy(t + 1, 1 - slot).start()
            w2_copy(t + 1, 1 - slot).start()

        @pl.when(t + 1 == steps)
        def _():
            wqkv_copy(0, 0).start()
            wp_copy.start()

        @pl.when(t == 2)
        def _():
            start(FC2_A)
            start(FC1_A)

        for i in range(images):
            pre = dot_nn(left[i], wbuf[slot]) + rows_ref[pl.ds(t, 1), :]
            hidden, slope = gelu_both(pre)
            hidden = hidden.astype(BF16)
            d_pre = (slope * dot_nt(right[i], wbuf[2 + slot])).astype(BF16)
            djoin[i, :, :width] = hidden
            djoin[i, :, width : 2 * width] = d_pre
            vec[pl.ds(7 + t, 1), :] += jnp.sum(d_pre.astype(F32), axis=0, keepdims=True)
            acc[i] += dot_nn(hidden, wbuf[2 + slot])
            dn2[i] += dot_nt(d_pre, wbuf[slot])

        tile[...] = dot_tn(column(0), flat(right))

        @pl.when(t == 2)
        def _():
            for k in (FC2_A, FC1_A):
                step_one(k)

        for k in range(2):

            @pl.when(t // 2 == k)
            def _():
                put_block_rows(k, t % 2)

        tile[...] = dot_tn(flat(left), column(1))
        for k in range(2):

            @pl.when(t // 2 == k)
            def _():
                put_folds(send_b.at[k], keep_b.at[k], t % 2)

    wqkv_copy(1, 1).start()
    wqkv_copy(2, 3).start()
    unit_in, att_in, rstd_in = fetch(unit_hbm, left), fetch(att_hbm, right), fetch(rstd_hbm, rstd_one)
    start(FC2_B)
    start(FC1_B)
    mid_in.wait()
    for i in range(images):
        gate = scal_ref[i, 5].astype(F32) * KEEP_SCALE
        final = mid[i] + gate * (acc[i] + rows_ref[4:5, :])
        out = jnp.where(row_valid(scal_ref, i, rows, half, 0), final, 0.0).astype(BF16)
        ost[i] = out[:half]
        gsend[i] = out[half:]
    out_own = pltpu.make_async_copy(ost, out_ref.at[pl.ds(x * images, images)], out_sem.at[0])
    out_own.start()
    out_far = Far(
        lambda: (gsend, out_ref.at[pl.ds(x * images, images)]), lambda: side_send.at[images], lambda: side_recv.at[images], across
    )

    wp_copy.wait()
    for i in range(images):
        live = row_valid(scal_ref, i, rows, half, 0)
        d_final = jnp.where(live, cot[i].astype(F32), 0.0)
        unit_two, rstd = norm_parts(mid[i])
        d_normed = dn2[i]
        vec[5:6, :] += jnp.sum(d_normed * unit_two, axis=0, keepdims=True)
        vec[6:7, :] += jnp.sum(d_normed, axis=0, keepdims=True)
        d_middle = d_final + norm_back(d_normed, rows_ref[7:8, :], unit_two, rstd)
        dn2[i] = d_middle
        gate = scal_ref[i, 4].astype(F32) * KEEP_SCALE
        d_branch = (d_middle * gate).astype(BF16)
        datt[i] = d_branch
        vec[4:5, :] += jnp.sum(d_branch.astype(F32), axis=0, keepdims=True)
    parcels[FC2_A].move(1)
    unit_in.wait()
    att_in.wait()
    rstd_in.wait()
    tile[...] = dot_tn(flat(right), flat(datt))
    put_folds(send_b.at[0], keep_b.at[2], 1)
    step_one(FC1_B)
    for i in range(images):
        datt[i] = dot_nt(datt[i], wbuf[2]).astype(BF16)
    step_one(FC2_B)

    low_lane = lax.broadcasted_iota(jnp.int32, (rows, 128), 1) < HEAD_DIM
    sides = (low_lane, jnp.logical_not(low_lane))
    cuts = lambda pair: [slice(k * width + 128 * pair, k * width + 128 * pair + 128) for k in range(3)]
    total_pairs = images * pairs

    def next_probs(index, slot):
        @pl.when(index + SLOTS < 2 * total_pairs)
        def _():
            probs_copy((index + SLOTS) % total_pairs, slot).start()

    def pump(plan, i, pair):
        for (image, at), job in plan.items():
            if at == pair:

                @pl.when(i == image)
                def _():
                    job()

    early_plan = {
        (0, 4): lambda: parcels[FC1_A].move(1),
        (2, 3): lambda: parcels[FC2_A].move(2),
    }

    @pl.loop(0, images)
    def _(i):
        for pair in range(pairs):
            index = i * pairs + pair
            slot = index % SLOTS
            probs_copy(index, slot).wait()
            q_cut, _, v_cut = cuts(pair)
            a2 = datt[i, :, q_cut]
            dv = dot_nn(probs[slot, 0], jnp.where(sides[0], a2, 0)) + dot_nn(probs[slot, 1], jnp.where(sides[1], a2, 0))
            djoin[i, :, v_cut] = dv.astype(BF16)
            next_probs(index, slot)
            pump(early_plan, i, pair)
        vec[3:4, :] += jnp.sum(djoin[i, :, 2 * width :].astype(F32), axis=0, keepdims=True)

    tile[...] = dot_tn(flat(left), column(2))
    put_folds(send_b.at[0], keep_b.at[2], 0)
    start(VAL_PROJ)

    plan = {
        (0, 5): lambda: parcels[FC1_B].move(1),
        (1, 0): lambda: step_one(VAL_PROJ),
        (1, 3): lambda: parcels[FC2_A].move(3),
        (1, 4): lambda: parcels[FC1_A].move(2),
        (2, 2): lambda: parcels[FC2_B].move(1),
        (2, 3): lambda: parcels[FC1_B].move(2),
    }

    @pl.loop(0, images)
    def _(i):
        q_slot = i % 2
        qkv_copy(i, q_slot).wait()
        for pair in range(pairs):
            index = total_pairs + i * pairs + pair
            slot = index % SLOTS
            probs_copy(index - total_pairs, slot).wait()
            q_cut, k_cut, v_cut = cuts(pair)
            q2, k2, v2, a2 = qkv[q_slot, :, q_cut], qkv[q_slot, :, k_cut], qkv[q_slot, :, v_cut], datt[i, :, q_cut]
            dq = dk = None
            for side in range(2):
                high = probs[slot, side].astype(F32)
                d_probs = dot_nt(v2, jnp.where(sides[side], a2, 0))
                inner = jnp.sum(high * d_probs, axis=0, keepdims=True)
                d_scores = (high * (d_probs - inner)).astype(BF16)
                parts = dot_tn(d_scores, jnp.where(sides[side], k2, 0)), dot_nn(d_scores, jnp.where(sides[side], q2, 0))
                dq, dk = parts if dq is None else (dq + parts[0], dk + parts[1])
            djoin[i, :, q_cut] = (dq * HEAD_DIM**-0.5).astype(BF16)
            djoin[i, :, k_cut] = dk.astype(BF16)
            next_probs(index, slot)
            pump(plan, i, pair)

        @pl.when(i + 2 < images)
        def _():
            qkv_copy(i + 2, q_slot).start()

        vec[2:3, :] += jnp.sum(djoin[i, :, :width].astype(F32), axis=0, keepdims=True)
        vec[0:1, :] += jnp.sum(djoin[i, :, width : 2 * width].astype(F32), axis=0, keepdims=True)

    for t, k in ((0, QUERY), (1, KEY)):
        tile[...] = dot_tn(flat(left), column(t))
        put_folds(send_c.at[t], keep_c.at[t], 0)
        start(k)
    wqkv_copy(0, 0).wait()
    wqkv_copy(1, 1).wait()
    wqkv_copy(2, 3).wait()
    out_far.wait()

    def input_grad(i):
        d_normed = dot_nt(djoin[i, :, :width], wbuf[0])
        d_normed += dot_nt(djoin[i, :, width : 2 * width], wbuf[1])
        d_normed += dot_nt(djoin[i, :, 2 * width :], wbuf[3])
        out = dn2[i] + norm_back(d_normed, rows_ref[5:6, :], left[i].astype(F32), rstd_one[i])
        acc[i, :half] = out[:half]
        gsend[i] = out[half:].astype(BF16)

    def exchange(k):
        return Far(lambda: (vec, vget.at[k]), lambda: vec_send.at[k], lambda: vec_recv.at[k], peers[k])

    def settle(k, trade):
        trade.wait()
        vec[...] += vget[k]

    def write_folds(total, ref, tile_at):
        for t in range(total.shape[1] // side_cols):
            for h in range(2):
                at = (tile_at + t) * width + h * side_cols
                ref[:, at : at + side_cols] = total[h * unit : h * unit + unit, t * side_cols : t * side_cols + side_cols]

    def write_fc2(total):
        fc2_ref[...] = total

    swaps = []

    def swap_out(i):
        swaps.append(
            Far(lambda: (gsend.at[i], grecv.at[i]), lambda: side_send.at[i], lambda: side_recv.at[i], across)
        )

    trade = exchange(0)
    input_grad(0)
    swap_out(0)
    settle(0, trade)
    trade = exchange(1)
    parcels[VAL_PROJ].move(1)
    step_one(QUERY)
    step_one(KEY)
    input_grad(1)
    swap_out(1)
    settle(1, trade)
    trade = exchange(2)
    parcels[QUERY].move(1)
    parcels[KEY].move(1)
    input_grad(2)
    swap_out(2)
    settle(2, trade)
    trade = exchange(3)
    grad_own = pltpu.make_async_copy(acc.at[:, pl.ds(0, half)], grad_ref, out_sem.at[1])
    grad_own.start()
    parcels[KEY].move(2)
    parcels[FC1_B].move(3)
    parcels[FC2_B].move(2)
    settle(3, trade)
    trade = exchange(4)
    parcels[FC2_A].finish(write_fc2)
    parcels[FC1_A].move(3)
    parcels[QUERY].move(2)
    parcels[VAL_PROJ].move(2)
    settle(4, trade)
    vec_ref[...] = vec[...]
    parcels[FC2_B].move(3)
    write_folds(parcels[FC1_B].gather(4), fc1_ref, 2)
    parcels[KEY].move(3)
    write_folds(parcels[FC1_A].gather(4), fc1_ref, 0)
    parcels[QUERY].move(3)
    parcels[VAL_PROJ].move(3)
    write_folds(parcels[KEY].gather(4), qkvg_ref, 1)
    parcels[FC2_B].finish(write_fc2)
    write_folds(parcels[QUERY].gather(4), qkvg_ref, 0)
    for copy in swaps:
        copy.wait()
    grad_oth = pltpu.make_async_copy(grecv, back_ref, out_sem.at[2])
    grad_oth.start()
    total = parcels[VAL_PROJ].gather(4)
    write_folds(total[:, :side_cols], qkvg_ref, 2)
    write_folds(total[:, side_cols:], projg_ref, 0)
    out_own.wait()
    grad_own.wait()
    grad_oth.wait()


def rest(facts, cotangent, cot_oth, n2, middle, qkv, probs, unit_one, rstd_one, attended, rows_in, w):
    images, half, width = cot_oth.shape
    rows = 2 * half
    hidden_width = w["fc1_weight"].shape[1]
    r, c = 2 * (width // GROUP), width
    fc2_rows = hidden_width // GROUP
    hbm = pl.BlockSpec(memory_space=pl.ANY)
    vmem = pl.BlockSpec(memory_space=pltpu.VMEM)
    smem = pl.BlockSpec(memory_space=pltpu.SMEM)
    dma = pltpu.SemaphoreType.DMA
    whole = lambda dtype: pltpu.VMEM((images, rows, width), dtype)
    half_block = lambda dtype: pltpu.VMEM((images, half, width), dtype)
    level_bufs = []
    for k, order in enumerate(ORDERS):
        names = "vyx" if k < 2 else "wvyx"
        block = (fc2_rows, width) if k < 2 else (r, c) if k < 5 else (r, c // 2)
        level_bufs += [pltpu.VMEM(shape, BF16) for shape in level_shapes(names, order, *block)]
    rows_of = lambda *lead: pltpu.VMEM(lead + (2, 2, 2, fc2_rows, width), BF16)
    folds_of = lambda count, cols: pltpu.VMEM((count, 2, 2, 2, 2, r, cols), BF16)
    return pl.pallas_call(
        rest_kernel,
        in_specs=[smem] * 4 + [hbm] * 13 + [vmem],
        out_specs=[vmem] * 5 + [hbm] * 3,
        out_shape=[
            jax.ShapeDtypeStruct((fc2_rows, width), F32),
            jax.ShapeDtypeStruct((r // 2, hidden_width), F32),
            jax.ShapeDtypeStruct((r // 2, 3 * width), F32),
            jax.ShapeDtypeStruct((r // 2, width), F32),
            jax.ShapeDtypeStruct((16, width), F32),
            jax.ShapeDtypeStruct((2 * images, half, width), BF16),
            jax.ShapeDtypeStruct((images, half, width), F32),
            jax.ShapeDtypeStruct((images, half, width), BF16),
        ],
        scratch_shapes=[
            whole(BF16), pltpu.VMEM((images, rows, 1), F32), whole(F32), whole(F32), whole(F32), whole(BF16), whole(BF16),
            pltpu.VMEM((4, width, width), BF16),
            pltpu.VMEM((2, rows, 3 * width), BF16),
            pltpu.VMEM((SLOTS, 2, rows, rows), BF16),
            pltpu.VMEM((images, rows, 3 * width), BF16),
            whole(BF16),
            pltpu.VMEM((width, width), F32),
            half_block(BF16), half_block(BF16), half_block(BF16),
            pltpu.VMEM((16, width), F32),
            pltpu.VMEM((5, 16, width), F32),
            rows_of(2), rows_of(), rows_of(),
            folds_of(3, c), folds_of(2, c), folds_of(2, c),
            folds_of(2, c // 2), folds_of(2, c // 2), folds_of(2, c // 2),
            *level_bufs,
            dma((8,)), dma((SLOTS,)), dma((2,)), dma((4,)), dma((PARTS, 5)), dma((PARTS, 5)), dma((images + 1,)),
            dma((images + 1,)), dma((5,)), dma((5,)), dma((3,)), pltpu.SemaphoreType.REGULAR((2,)),
        ],
        compiler_params=pltpu.CompilerParams(collective_id=0, has_side_effects=True, vmem_limit_bytes=64 * MIB),
        name="rest",
    )(*facts, cotangent, cot_oth, n2, middle, qkv, probs, w["fc1_weight"], w["fc2_weight"], w["proj_weight"],
      w["qkv_weight"], unit_one, rstd_one, attended, rows_in)


def spread(value):
    return lax.psum_scatter(value, ("img", "seq"), scatter_dimension=0, tiled=True)


def unfold(send, keep, core, folds):
    rows, cols = send.shape[-2], send.shape[-1]
    send, keep = (v.reshape(GROUP // 4, 2, rows, cols) for v in (send, keep))
    both = jnp.stack([jnp.where(core == 0, keep, send), jnp.where(core == 0, send, keep)], axis=1).astype(F32)
    if folds == 1:
        return both.reshape(GROUP * rows, cols)
    tiles = 4
    both = both.reshape(GROUP, 2, rows // 2, tiles, cols // tiles)
    return both.transpose(0, 2, 3, 1, 4).reshape(GROUP * rows // 2, 2 * cols)


def swap(value, axis, bit, size):
    return lax.ppermute(value, axis, [(i, i ^ bit) for i in range(size)])


def shards(img_size, args):
    (patches, grid_shape, split_rows, owner_shard, drop_masks, ln1_gain, ln1_bias, qkv_weight, qv_bias, proj_weight,
     proj_bias, ln2_gain, ln2_bias, fc1_weight, fc1_bias, fc2_weight, fc2_bias, cotangent) = args
    all_images, _, half, width = patches.shape
    images = all_images // 2
    rows = 2 * half
    tokens = images * rows
    side = lax.axis_index("seq")
    line = lax.axis_index("img")
    owners = 2 * img_size
    row = lambda v: v.reshape(1, -1)
    w = dict(
        ln1_gain=row(ln1_gain), ln1_bias=row(ln1_bias), qkv_weight=qkv_weight, q_bias=row(qv_bias[:width]),
        v_bias=row(qv_bias[width:]), proj_weight=proj_weight, proj_bias=row(proj_bias), ln2_gain=row(ln2_gain),
        ln2_bias=row(ln2_bias), fc1_weight=fc1_weight, fc1_bias=row(fc1_bias), fc2_weight=fc2_weight, fc2_bias=row(fc2_bias),
    )

    def exchange(value):
        value = value.reshape(all_images, half, width)
        own = lax.dynamic_slice_in_dim(value, side * images, images, axis=0)
        away = lax.dynamic_slice_in_dim(value, (1 - side) * images, images, axis=0)
        return own, swap(away, "seq", 1, 2)

    def place(own, back):
        back = back.astype(own.dtype)
        first = jnp.where(side == 0, own, back)
        second = jnp.where(side == 0, back, own)
        return jnp.concatenate([first, second], axis=0).reshape(all_images, 1, half, width)

    def restore(own, oth):
        return place(own, swap(oth, "seq", 1, 2))

    across = grid_shape[:, 1]
    counts = jnp.stack([split_rows * across, (grid_shape[:, 0] - split_rows) * across], axis=0)
    count_own = jnp.where(side == 0, counts[0], counts[1])
    count_oth = jnp.where(side == 0, counts[1], counts[0])
    special = (owner_shard == side).astype(jnp.int32)
    table = jnp.stack([count_own, special, count_oth, 1 - special, drop_masks[:, 0], drop_masks[:, 1]], axis=1)
    scal = lax.dynamic_slice_in_dim(table, side * images, images, axis=0)

    flat = lambda v: v.reshape(tokens, v.shape[-1])
    unit1 = width // GROUP
    unit2 = fc2_weight.shape[0] // GROUP
    if owners == GROUP:
        merge = lambda v: v.reshape(all_images, half, width)
        facts = (grid_shape, split_rows, owner_shard, drop_masks)
        unit_one, rstd_one, qkv, probs, attended, middle, n2, rows_in, c_oth = opening(
            facts, merge(patches), merge(cotangent),
            (ln1_gain, ln1_bias, qv_bias, proj_bias, ln2_gain, ln2_bias, fc1_bias, fc2_bias, qkv_weight, proj_weight),
        )
        fc2_part, fc1_part, u_part, proj_part, sums, out_part, grad_own, grad_back = rest(
            facts, merge(cotangent), c_oth, n2, middle, qkv, probs, unit_one, rstd_one, attended, rows_in, w
        )
        outs = emit(
            fc2_part, fc1_part, u_part, proj_part, sums, rows_in, qkv_weight,
            grad_own, grad_back, out_part,
        )
        layer_out, patches_grad = (v.reshape(all_images, 1, half, width) for v in outs[:2])
        return (layer_out, patches_grad, *outs[2:])
    else:
        x_own, x_oth = exchange(patches)
        c_own, c_oth = exchange(cotangent)
        n1, qkv, probs, attended, middle, n2 = front(scal, x_own, x_oth, w)
        mine = lax.rem(line, 2).reshape(1)
        hidden, slope, out_own, out_oth = mlp(scal, flat(n2), flat(middle), w, images, 512)
        layer_out = restore(out_own, out_oth)
        dn2, s2, k2, s1, k1, fc2_bias_grad, fc1_bias_grad = mlp_back(
            scal, mine, c_own, c_oth, flat(n2), hidden, slope, w, unit1, unit2
        )
        dn2 = dn2.reshape(images, rows, width)
        d_middle, d_branch, d_join, ln2_gain_grad, ln2_bias_grad, proj_bias_grad, q_grad, v_grad = attend_back(
            scal, c_own, c_oth, dn2, middle, qkv, probs, w
        )
        st, kt, grad_own, grad_oth, ln1_gain_grad, ln1_bias_grad = tail(
            mine, flat(n1), flat(d_join), flat(attended), flat(d_branch), x_own, x_oth, flat(d_middle), w, unit1
        )
        patches_grad = restore(grad_own, grad_oth)
        vectors = (
            ln1_gain_grad, ln1_bias_grad, jnp.concatenate([q_grad, v_grad], axis=1), proj_bias_grad, ln2_gain_grad,
            ln2_bias_grad, fc1_bias_grad, fc2_bias_grad,
        )
        fc2_grad = spread(unfold(s2, k2, line % 2, 1))
        fc1_grad = spread(unfold(s1, k1, line % 2, 2))
        tail_grad = spread(unfold(st, kt, line % 2, 2))
        qkv_grad, proj_grad = tail_grad[:, : 3 * width], tail_grad[:, 3 * width :]
        pieces = [spread(v.reshape(-1)) for v in vectors]
    l1g, l1b, qvb, pjb, l2g, l2b, f1b, f2b = pieces
    return (
        layer_out, patches_grad, l1g, l1b, qkv_grad, qvb, proj_grad, pjb, l2g, l2b, fc1_grad, f1b, fc2_grad, f2b,
    )


def solution(mesh):
    rep = [P()] * 12
    vec = P(("img", "seq"))
    mat = P(("img", "seq"), None)
    rows = P("img", "seq", None, None)

    def run(*args):
        return shards(mesh.shape["img"], args)

    return jax.shard_map(
        run,
        mesh=mesh,
        in_specs=(rows, P("img", None), P("img"), P("img"), P("img", None), *rep, rows),
        out_specs=(rows, rows, vec, vec, mat, vec, mat, vec, vec, vec, mat, vec, mat, vec),
        check_vma=False,
    )
```

profile of v0, /device:TPU:0, one launch (start us, length us, event | category | flops | bytes accessed | tf_op | source)
XLA Modules:
  0.0 173.3 jit_solution(10919986734074145632)
XLA Ops:
  0.6 1.4 copy.34.grid_ref
  2.0 1.4 copy.35.drop_ref
  3.3 39.6 %opening.1 = (bf16[3,320,768]{2,1,0:T(8,128)(2,1)}, f32[3,320,1]{2,1,0:T(8,128)}, bf16[3,320,2304]{2,1,0:T(8,128)(2,1)}, bf16[3,12,320,320]{3,2,1,0:T(8,128)(2,1...) custom-call(s32[6,2]{1,0:T(8,128)} %copy.34.grid_ref, ...), custom_call_target="tpu_custom_call" | custom-call | tf_op jit(solution)/shard_map/opening/pallas_call | solution.py:608
  43.0 124.6 %rest.1 = (f32[96,768]{1,0:T(8,128)}, f32[24,3072]{1,0:T(8,128)}, f32[24,2304]{1,0:T(8,128)}, f32[24,768]{1,0:T(8,128)}, f32[16,768]{1,0:T(8,128)}, /*index=5*/b...) custom-call(s32[6,2]{1,0:T(8,128)} %copy.34.grid_ref, s32[6]{0:T(128)} %split_ref.3, ...), custom_call_target="tpu_custom_call" | custom-call | tf_op jit(solution)/shard_map/rest/pallas_call | solution.py:1253
  167.6 5.5 %emit.1 = (bf16[6,160,768]{2,1,0:T(8,128)(2,1)}, f32[6,160,768]{2,1,0:T(8,128)}, f32[24]{0:T(128)}, f32[24]{0:T(128)}, f32[24,2304]{1,0:T(8,128)}, /*index=5*/f3...) custom-call(f32[96,768]{1,0:T(8,128)} %get-tuple-element.54.fc2_ref,, ...), custom_call_target="tpu_custom_call" | custom-call | tf_op jit(solution)/shard_map/emit/pallas_call | solution.py:698
where the time goes:
time: 176 us; the launch traced here: 173 us
  Pallas kernels  170 us (97%)
  local copies, waits for them, and re-layouts  2.7 us (2%)
    pallas_call x1, Pallas kernels, rest(): pl.pallas_call(rest_kernel, in_specs=[smem] * 4 + [hbm] * 13 + [vmem], ou...  125 us
    pallas_call x1, Pallas kernels, opening(): pl.pallas_call(open_kernel, grid=(images,), in_specs=[pl.BlockSpec(memory...  39.6 us
    pallas_call x1, Pallas kernels, emit(): pl.pallas_call(emit_kernel, grid=(1,), in_specs=[whole(v) for v in (fc2,...  5.49 us

commit v1 on v0

--- a/solution.py
+++ b/solution.py
@@ -57,13 +57,13 @@
         image, k = key
         at = self.x * self.images + image
         if k >= 4:
-            return self.drop[at, k - 4]
+            return self.drop[k - 4, at]
         if k % 2 == 1:
             own = (self.owner[at] == self.x).astype(jnp.int32)
             return own if k == 1 else 1 - own
-        across = self.grid[at, 1]
+        across = self.grid[1, at]
         first = self.split[at] * across
-        second = (self.grid[at, 0] - self.split[at]) * across
+        second = (self.grid[0, at] - self.split[at]) * across
         return jnp.where(self.x == k // 2, first, second)
 
 
@@ -494,141 +494,8 @@
     )(mine, n1, d_join, attended, d_branch, w["qkv_weight"], own, oth, d_middle, w["ln1_gain"])
 
 
-def open_kernel(
-    grid_ref, split_ref, owner_ref, drop_ref, patches_ref, cot_ref, g1_ref, b1_ref, qv_ref, pb_ref, g2_ref, b2_ref, c1_ref, c2_ref, wqkv_hbm, wp_hbm,
-    unit_ref, rstd_ref, qkv_ref, probs_ref, att_ref, mid_ref, n2_ref, rows_ref, cot_oth,
-    xbuf, wqkv_ref, wp_ref, load_sem, send_sem, recv_sem,
-):
-    image = pl.program_id(0)
-    images, rows, width = xbuf.shape
-    half = rows // 2
-    line = lax.axis_index("img")
-    x_at = lax.axis_index("seq")
-    across = (line, 1 - x_at)
-    scal_ref = Facts((grid_ref, split_ref, owner_ref, drop_ref), images, x_at)
-    loads = [
-        pltpu.make_async_copy(wqkv_hbm, wqkv_ref, load_sem.at[0]),
-        pltpu.make_async_copy(wp_hbm, wp_ref, load_sem.at[1]),
-    ]
-
-    def own_copy(i):
-        return pltpu.make_async_copy(patches_ref.at[x_at * images + i], xbuf.at[i, pl.ds(0, half)], load_sem.at[2 + i])
-
-    def far_copy(i):
-        return pltpu.make_async_remote_copy(
-            src_ref=patches_ref.at[(1 - x_at) * images + i], dst_ref=xbuf.at[i, pl.ds(half, half)],
-            send_sem=send_sem.at[i], recv_sem=recv_sem.at[i], device_id=across, device_id_type=MESH,
-        )
-
-    def cot_copy():
-        return pltpu.make_async_remote_copy(
-            src_ref=cot_ref.at[pl.ds((1 - x_at) * images, images)], dst_ref=cot_oth,
-            send_sem=send_sem.at[images], recv_sem=recv_sem.at[images], device_id=across, device_id_type=MESH,
-        )
-
-    @pl.when(image == 0)
-    def _():
-        barrier = pltpu.get_barrier_semaphore()
-        pl.semaphore_signal(barrier, inc=1, device_id=across, device_id_type=MESH)
-        own_copy(0).start()
-        loads[0].start()
-        pl.semaphore_wait(barrier, 1)
-        for i in range(images):
-            far_copy(i).start()
-        for i in range(1, images):
-            own_copy(i).start()
-        loads[1].start()
-        row = lambda ref: ref[...].reshape(1, -1)
-        rows_ref[...] = jnp.zeros_like(rows_ref)
-        for k in range(c1_ref.shape[0] // width):
-            rows_ref[k : k + 1, :] = row(c1_ref)[:, k * width : k * width + width]
-        for k, ref in enumerate((c2_ref, g1_ref, b1_ref, g2_ref, b2_ref, pb_ref)):
-            rows_ref[4 + k : 5 + k, :] = row(ref)
-        rows_ref[10:11, :] = row(qv_ref)[:, :width]
-        rows_ref[11:12, :] = row(qv_ref)[:, width:]
-        loads[0].wait()
-        loads[1].wait()
-
-    for i in range(images):
-
-        @pl.when(image == i)
-        def _():
-            own_copy(i).wait()
-            far_copy(i).wait()
-
-    @pl.when(image == 1)
-    def _():
-        cot_copy().start()
-
-    vector = lambda k: rows_ref[k : k + 1, :]
-    unit, rstd = norm_parts(xbuf[image].astype(F32))
-    unit_ref[0] = unit.astype(BF16)
-    rstd_ref[0] = rstd
-    n1 = (unit * vector(5) + vector(6)).astype(BF16)
-    qkv_ref[0, :, :width] = ((dot_nn(n1, wqkv_ref[:, :width]) + vector(10)).astype(BF16) * BF16(HEAD_DIM**-0.5))
-    qkv_ref[0, :, width : 2 * width] = dot_nn(n1, wqkv_ref[:, width : 2 * width]).astype(BF16)
-    qkv_ref[0, :, 2 * width :] = (dot_nn(n1, wqkv_ref[:, 2 * width :]) + vector(11)).astype(BF16)
-    fill = jnp.where(row_valid(scal_ref, image, rows, half, 0), 0.0, MASK_FILL)
-    low_lane = lax.broadcasted_iota(jnp.int32, (rows, 128), 1) < HEAD_DIM
-    for pair in range(width // 128):
-        cut, k_cut, v_cut = (slice(k * width + 128 * pair, k * width + 128 * pair + 128) for k in range(3))
-        q2, k2, v2 = qkv_ref[0, :, cut], qkv_ref[0, :, k_cut], qkv_ref[0, :, v_cut]
-        total = None
-        for side in range(2):
-            mine = low_lane if side == 0 else jnp.logical_not(low_lane)
-            scores = dot_nt(k2, jnp.where(mine, q2, 0)) + fill
-            top = jnp.max(scores, axis=0, keepdims=True)
-            weight = jnp.exp(scores - top)
-            probs = (weight * (1.0 / jnp.sum(weight, axis=0, keepdims=True))).astype(BF16)
-            probs_ref[0, 2 * pair + side] = probs
-            part = dot_tn(probs, jnp.where(mine, v2, 0))
-            total = part if total is None else total + part
-        att_ref[0, :, cut] = total.astype(BF16)
-    keep = scal_ref[image, 4].astype(F32) * KEEP_SCALE
-    middle = xbuf[image].astype(F32) + keep * (dot_nn(att_ref[0], wp_ref[...]) + vector(9))
-    mid_ref[0] = middle
-    unit, _ = norm_parts(middle)
-    n2_ref[0] = (unit * vector(7) + vector(8)).astype(BF16)
-
-    @pl.when(image == images - 1)
-    def _():
-        cot_copy().wait()
-
-
-def opening(facts, patches, cotangent, args):
-    all_images, half, width = patches.shape
-    images = all_images // 2
-    rows = 2 * half
-    heads = width // HEAD_DIM
-    per = lambda *tail: pl.BlockSpec((1,) + tail, lambda i: (i,) + (0,) * len(tail))
-    hbm = pl.BlockSpec(memory_space=pl.ANY)
-    vmem = pl.BlockSpec(memory_space=pltpu.VMEM)
-    dma = pltpu.SemaphoreType.DMA
-    shape = jax.ShapeDtypeStruct
-    return pl.pallas_call(
-        open_kernel,
-        grid=(images,),
-        in_specs=[pl.BlockSpec(memory_space=pltpu.SMEM)] * 4 + [hbm, hbm] + [vmem] * 8 + [hbm, hbm],
-        out_specs=[
-            per(rows, width), per(rows, 1), per(rows, 3 * width), per(heads, rows, rows), per(rows, width),
-            per(rows, width), per(rows, width), vmem, hbm,
-        ],
-        out_shape=[
-            shape((images, rows, width), BF16), shape((images, rows, 1), F32), shape((images, rows, 3 * width), BF16),
-            shape((images, heads, rows, rows), BF16), shape((images, rows, width), BF16), shape((images, rows, width), F32),
-            shape((images, rows, width), BF16), shape((16, width), F32), shape((images, half, width), BF16),
-        ],
-        scratch_shapes=[
-            pltpu.VMEM((images, rows, width), BF16), pltpu.VMEM((width, 3 * width), BF16), pltpu.VMEM((width, width), BF16),
-            dma((2 + images,)), dma((images + 1,)), dma((images + 1,)),
-        ],
-        compiler_params=pltpu.CompilerParams(collective_id=1, has_side_effects=True, vmem_limit_bytes=63 * MIB),
-        name="opening",
-    )(*facts, patches, cotangent, *args)
-
-
 def emit_kernel(
-    fc2_ref, fc1_ref, u_ref, proj_ref, sums_ref, rows_ref, w_ref, own_ref, back_ref, lo_ref,
+    fc2_ref, fc1_ref, u_ref, proj_ref, sums_ref, gain_ref, bias_ref, w_ref, own_ref, back_ref, lo_ref,
     out_ref, grad_ref, l1g, l1b, qkvg, qvb, projg, pjb, l2g, l2b, fc1g, f1b, fc2g, f2b, buf, own_buf, back_buf, lo_buf, sems,
 ):
     side = lax.axis_index("seq")
@@ -657,8 +524,8 @@
     lane = lax.broadcasted_iota(jnp.int32, (unit, width), 1)
     slot = lax.broadcasted_iota(jnp.int32, (unit, width), 0)
     here = lane == owner * unit + slot
-    column = lambda k: jnp.sum(jnp.where(here, rows_ref[k : k + 1, :], 0.0), axis=1, keepdims=True)
-    gain, bias = column(5), column(6)
+    column = lambda ref: jnp.sum(jnp.where(here, ref[...].reshape(1, width), 0.0), axis=1, keepdims=True)
+    gain, bias = column(gain_ref), column(bias_ref)
     gain_sum = bias_sum = 0.0
     for k, at in enumerate((2, 0, 3)):
         cut = slice(k * width, k * width + width)
@@ -685,7 +552,7 @@
     other.wait()
 
 
-def emit(fc2, fc1, u, proj, sums, rows, qkv_weight, own, back, layer_out):
+def emit(fc2, fc1, u, proj, sums, gain, bias, qkv_weight, own, back, layer_out):
     images, half, width = own.shape
     unit = u.shape[0]
     hbm = pl.BlockSpec(memory_space=pl.ANY)
@@ -698,7 +565,7 @@
     return pl.pallas_call(
         emit_kernel,
         grid=(1,),
-        in_specs=[whole(v) for v in (fc2, fc1, u, proj, sums, rows)]
+        in_specs=[whole(v) for v in (fc2, fc1, u, proj, sums, gain, bias)]
         + [pl.BlockSpec((unit, 3 * width), lambda i: (2 * lax.axis_index("img") + lax.axis_index("seq"), 0)), hbm, hbm, hbm],
         out_specs=[hbm, hbm] + [whole(v) for v in outs],
         scratch_shapes=[
@@ -708,7 +575,7 @@
         out_shape=[jax.ShapeDtypeStruct(layer_out.shape, BF16), shape(2 * images, half, width)] + outs,
         compiler_params=pltpu.CompilerParams(vmem_limit_bytes=63 * MIB),
         name="emit",
-    )(fc2, fc1, u, proj, sums, rows, qkv_weight, own, back, layer_out)
+    )(fc2, fc1, u, proj, sums, gain, bias, qkv_weight, own, back, layer_out)
 
 
 MESH = pl.DeviceIdType.MESH
@@ -815,19 +682,39 @@
     ]
 
 
-ORDERS = ("yvxw", "vxyw", "xwyv", "yxwv", "vwyx", "yvxw", "vywx")
+ORDERS = ("yvxw", "yvxw", "wxvy", "xwvy", "yvwx", "yvwx", "vyxw")
 FC2_A, FC2_B, FC1_A, FC1_B, VAL_PROJ, QUERY, KEY = range(7)
+PLAN = {
+    "b02": ((FC2_B, 0),),
+    "b24": ((FC1_B, 0),),
+    "c01": ((FC2_A, 1),),
+    "c04": ((VAL_PROJ, 0),),
+    "c12": ((FC2_B, 1),),
+    "c15": ((FC2_A, 2),),
+    "c20": ((FC1_A, 1),),
+    "c22": ((FC1_B, 1),),
+    "c25": ((FC2_A, 3), (FC2_B, 2), (VAL_PROJ, 1)),
+    "key": ((QUERY, 0),),
+    "input0": ((KEY, 0), (FC2_B, 3)),
+    "input1": ((VAL_PROJ, 2), (QUERY, 1)),
+    "input2": ((FC1_A, 2), (FC2_A, 4), (KEY, 1)),
+    "end0": ((FC2_B, 4), (FC1_B, 2), (QUERY, 2), (KEY, 2)),
+    "end1": (
+        (FC1_A, 3), (VAL_PROJ, 3), (FC1_B, 3), (KEY, 3), (QUERY, 3), (FC1_A, 4), (VAL_PROJ, 4), (FC1_B, 4), (QUERY, 4),
+        (KEY, 4),
+    ),
+}
 
 
 def rest_kernel(
-    grid_ref, split_ref, owner_ref, drop_ref, cot_hbm, cot_oth, n2_hbm, mid_hbm, qkv_hbm, probs_hbm, w1_hbm, w2_hbm, wp_hbm, wqkv_hbm, unit_hbm, rstd_hbm,
-    att_hbm, rows_ref,
-    fc2_ref, fc1_ref, qkvg_ref, projg_ref, vec_ref, out_ref, grad_ref, back_ref,
-    cot, rstd_one, dn2, mid, acc, left, right, wbuf, qkv, probs, djoin, datt, tile, ost, gsend, grecv, vec, vget,
+    grid_ref, split_ref, owner_ref, drop_ref, patches_hbm, cot_hbm, w1_hbm, w2_hbm, wp_hbm, wqkv_hbm,
+    g1_ref, b1_ref, qv_ref, pb_ref, g2_ref, b2_ref, c1_ref, c2_ref,
+    fc2_ref, fc1_ref, qkvg_ref, projg_ref, vec_ref, out_ref, grad_ref, back_ref, unit_hbm, qkv_hbm, probs_hbm, att_hbm,
+    cot, rstd_one, rows_ref, dn2, mid, acc, left, right, wbuf, qkv, probs, djoin, datt, tile, ost, gsend, grecv, vec, vget,
     keep_a, send_a, land_a, keep_b, send_b, land_b, keep_c, send_c, land_c, *others,
 ):
     levels = [others[4 * k : 4 * k + 4] for k in range(PARTS)]
-    (load_sem, probs_sem, qkv_sem, w_sem, send_sem, recv_sem, side_send, side_recv, vec_send, vec_recv, out_sem,
+    (load_sem, probs_sem, qkv_sem, w_sem, open_sem, open_send, open_recv, send_sem, recv_sem, side_send, side_recv, vec_send, vec_recv, out_sem,
      free_sem) = others[4 * PARTS :]
     images, rows, width = dn2.shape
     half = rows // 2
@@ -874,14 +761,184 @@
         at = pl.multiple_of(t * width, 128)
         return pltpu.make_async_copy(w2_hbm.at[pl.ds(at, width), :], wbuf.at[2 + slot], w_sem.at[2 + slot])
 
-    first = [fetch(cot_hbm.at[pl.ds(x * images, images)], cot.at[:, pl.ds(0, half)]), fetch(cot_oth, cot.at[:, pl.ds(half, half)]), fetch(n2_hbm, left)]
-    w1_copy(0, 0).start()
-    w2_copy(0, 0).start()
-    mid_in = fetch(mid_hbm, mid)
+    def x_copy(i):
+        return pltpu.make_async_copy(patches_hbm.at[x * images + i], right.at[i, pl.ds(0, half)], open_sem.at[i])
+
+    def x_far(i):
+        return pltpu.make_async_remote_copy(
+            src_ref=patches_hbm.at[(1 - x) * images + i], dst_ref=right.at[i, pl.ds(half, half)],
+            send_sem=open_send.at[i], recv_sem=open_recv.at[i], device_id=across, device_id_type=MESH,
+        )
+
+    def cot_far(i):
+        return pltpu.make_async_remote_copy(
+            src_ref=cot_hbm.at[(1 - x) * images + i], dst_ref=cot.at[i, pl.ds(half, half)],
+            send_sem=open_send.at[images + i], recv_sem=open_recv.at[images + i], device_id=across, device_id_type=MESH,
+        )
+
+    def probs_out(index, slot):
+        return pltpu.make_async_copy(
+            probs.at[slot], probs_hbm.at[index // pairs, pl.ds(2 * (index % pairs), 2)], probs_sem.at[slot]
+        )
+
+    def saves(i):
+        return [
+            pltpu.make_async_copy(datt.at[i], unit_hbm.at[i], open_sem.at[images + 4 * i]),
+            pltpu.make_async_copy(djoin.at[i], qkv_hbm.at[i], open_sem.at[images + 4 * i + 1]),
+            pltpu.make_async_copy(ost.at[i], att_hbm.at[i, pl.ds(0, half)], open_sem.at[images + 4 * i + 2]),
+            pltpu.make_async_copy(gsend.at[i], att_hbm.at[i, pl.ds(half, half)], open_sem.at[images + 4 * i + 3]),
+        ]
+
+    def wqkv_copy(k, slot):
+        return pltpu.make_async_copy(wqkv_hbm.at[:, pl.ds(k * width, width)], wbuf.at[slot], w_sem.at[slot])
+
+    def wp_copy(slot):
+        return pltpu.make_async_copy(wp_hbm, wbuf.at[slot], w_sem.at[slot])
+
+    def write_folds(total, ref, tile_at):
+        for t in range(total.shape[1] // side_cols):
+            for h in range(2):
+                at = (tile_at + t) * width + h * side_cols
+                ref[:, at : at + side_cols] = total[h * unit : h * unit + unit, t * side_cols : t * side_cols + side_cols]
+
+    def write_fc2(total):
+        fc2_ref[...] = total
+
+    def write_out(k):
+        if k in (FC2_A, FC2_B):
+            return parcels[k].finish(write_fc2)
+        total = parcels[k].gather(4)
+        if k == VAL_PROJ:
+            write_folds(total[:, :side_cols], qkvg_ref, 2)
+            write_folds(total[:, side_cols:], projg_ref, 0)
+        else:
+            ref, tile_at = {FC1_A: (fc1_ref, 0), FC1_B: (fc1_ref, 2), QUERY: (qkvg_ref, 0), KEY: (qkvg_ref, 1)}[k]
+            write_folds(total, ref, tile_at)
+
+    def at_point(name):
+        for k, step in PLAN.get(name, ()):
+            if step == 0:
+                step_one(k)
+            elif step < 4:
+                parcels[k].move(step)
+            else:
+                write_out(k)
+
+    def plan_of(tag):
+        return {
+            (int(name[1]), int(name[2])): (lambda name=name: at_point(name))
+            for name in PLAN if len(name) == 3 and name[0] == tag and name[1:].isdigit()
+        }
+
+    def pump(plan, i, pair):
+        for (image, at), job in plan.items():
+            if at == pair:
+
+                @pl.when(i == image)
+                def _():
+                    job()
+
+    first_plan = {
+        (0, 3): lambda: x_far(2).start(),
+        (1, 1): lambda: cot_far(0).start(),
+        (2, 3): lambda: cot_far(2).start(),
+    }
+    weights_in = [wqkv_copy(0, 0), wqkv_copy(1, 2), wqkv_copy(2, 3), wp_copy(1)]
+    x_copy(0).start()
+    pl.semaphore_wait(barrier, len(peers))
+    x_far(0).start()
+    for copy in weights_in:
+        copy.start()
+    for i in range(1, images):
+        x_copy(i).start()
+    cot_in = fetch(cot_hbm.at[pl.ds(x * images, images)], cot.at[:, pl.ds(0, half)])
+    line_of = lambda ref: ref[...].reshape(1, -1)
+    for k in range(steps):
+        rows_ref[k : k + 1, :] = line_of(c1_ref)[:, k * width : k * width + width]
+    for k, ref in enumerate((c2_ref, g1_ref, b1_ref, g2_ref, b2_ref, pb_ref)):
+        rows_ref[4 + k : 5 + k, :] = line_of(ref)
+    rows_ref[10:11, :] = line_of(qv_ref)[:, :width]
+    rows_ref[11:12, :] = line_of(qv_ref)[:, width:]
+    vector = lambda k: rows_ref[k : k + 1, :]
+    low_lane = lax.broadcasted_iota(jnp.int32, (rows, 128), 1) < HEAD_DIM
+    sides = (low_lane, jnp.logical_not(low_lane))
+    cuts = lambda pair: [slice(k * width + 128 * pair, k * width + 128 * pair + 128) for k in range(3)]
+    vec[...] = jnp.zeros_like(vec)
+    acc[...] = jnp.zeros_like(acc)
+    dn2[...] = jnp.zeros_like(dn2)
+    for copy in weights_in:
+        copy.wait()
+
+    @pl.loop(0, images)
+    def _(i):
+        x_copy(i).wait()
+        x_far(i).wait()
+
+        @pl.when(i == 0)
+        def _():
+            x_far(1).start()
+
+        @pl.when(i == images - 1)
+        def _():
+            cot_far(1).start()
+
+        unit_one, rstd = norm_parts(right[i].astype(F32))
+        datt[i] = unit_one.astype(BF16)
+        rstd_one[i] = rstd
+        n1 = (unit_one * vector(5) + vector(6)).astype(BF16)
+        djoin[i, :, :width] = (dot_nn(n1, wbuf[0]) + vector(10)).astype(BF16) * BF16(HEAD_DIM**-0.5)
+        djoin[i, :, width : 2 * width] = dot_nn(n1, wbuf[2]).astype(BF16)
+        djoin[i, :, 2 * width :] = (dot_nn(n1, wbuf[3]) + vector(11)).astype(BF16)
+
+        @pl.when(i == images - 1)
+        def _():
+            w1_copy(0, 0).start()
+            w2_copy(0, 0).start()
+
+        fill = jnp.where(row_valid(scal_ref, i, rows, half, 0), 0.0, MASK_FILL)
+        for pair in range(pairs):
+            index = i * pairs + pair
+            slot = index % SLOTS
+
+            @pl.when(index >= SLOTS)
+            def _():
+                probs_out(index - SLOTS, slot).wait()
+
+            q_cut, k_cut, v_cut = cuts(pair)
+            q2, k2, v2 = djoin[i, :, q_cut], djoin[i, :, k_cut], djoin[i, :, v_cut]
+            total = None
+            for side in range(2):
+                scores = dot_nt(k2, jnp.where(sides[side], q2, 0)) + fill
+                top = jnp.max(scores, axis=0, keepdims=True)
+                weight = jnp.exp(scores - top)
+                low = (weight * (1.0 / jnp.sum(weight, axis=0, keepdims=True))).astype(BF16)
+                probs[slot, side] = low
+                part = dot_tn(low, jnp.where(sides[side], v2, 0))
+                total = part if total is None else total + part
+            attended = total.astype(BF16)
+            ost[i, :, q_cut] = attended[:half]
+            gsend[i, :, q_cut] = attended[half:]
+            probs_out(index, slot).start()
+            pump(first_plan, i, pair)
+        gate = scal_ref[i, 4].astype(F32) * KEEP_SCALE
+        attended = jnp.concatenate([ost[i], gsend[i]], axis=0)
+        middle = right[i].astype(F32) + gate * (dot_nn(attended, wbuf[1]) + vector(9))
+        mid[i] = middle
+        unit_two, _ = norm_parts(middle)
+        left[i] = (unit_two * vector(7) + vector(8)).astype(BF16)
+        for copy in saves(i):
+            copy.start()
+
+    for slot in range(SLOTS):
+        probs_out(images * pairs - SLOTS + slot, slot).wait()
+    for i in range(images):
+        for copy in saves(i):
+            copy.wait()
     for slot in range(SLOTS):
         probs_copy(slot, slot).start()
     for slot in range(2):
         qkv_copy(slot, slot).start()
+    cot_in.wait()
 
     place = {
         "core": (core, sibling), "y": (y, level, 1 - y), "x": (x, across, 1 - x),
@@ -946,24 +1003,6 @@
     flat = lambda ref: ref[...].reshape(images * rows, ref.shape[-1])
     column = lambda k: djoin[:, :, k * width : k * width + width].reshape(images * rows, width)
 
-    vec[...] = jnp.zeros_like(vec)
-    acc[...] = jnp.zeros_like(acc)
-    dn2[...] = jnp.zeros_like(dn2)
-    for copy in first:
-        copy.wait()
-    for i in range(images):
-        gate = scal_ref[i, 5].astype(F32) * KEEP_SCALE
-        live = row_valid(scal_ref, i, rows, half, 0)
-        d_mlp = (jnp.where(live, cot[i].astype(F32), 0.0) * gate).astype(BF16)
-        right[i] = d_mlp
-        vec[11:12, :] += jnp.sum(d_mlp.astype(F32), axis=0, keepdims=True)
-    pl.semaphore_wait(barrier, len(peers))
-
-    wp_copy = pltpu.make_async_copy(wp_hbm, wbuf.at[2], w_sem.at[2])
-
-    def wqkv_copy(k, slot):
-        return pltpu.make_async_copy(wqkv_hbm.at[:, pl.ds(k * width, width)], wbuf.at[slot], w_sem.at[slot])
-
     @pl.loop(0, steps)
     def _(t):
         slot = t % 2
@@ -978,7 +1017,7 @@
         @pl.when(t + 1 == steps)
         def _():
             wqkv_copy(0, 0).start()
-            wp_copy.start()
+            wp_copy(2).start()
 
         @pl.when(t == 2)
         def _():
@@ -986,14 +1025,26 @@
             start(FC1_A)
 
         for i in range(images):
-            pre = dot_nn(left[i], wbuf[slot]) + rows_ref[pl.ds(t, 1), :]
-            hidden, slope = gelu_both(pre)
+            hidden, slope = gelu_both(dot_nn(left[i], wbuf[slot]) + rows_ref[pl.ds(t, 1), :])
             hidden = hidden.astype(BF16)
-            d_pre = (slope * dot_nt(right[i], wbuf[2 + slot])).astype(BF16)
             djoin[i, :, :width] = hidden
+            djoin[i, :, 2 * width :] = slope.astype(BF16)
+            acc[i] += dot_nn(hidden, wbuf[2 + slot])
+
+        @pl.when(t == 0)
+        def _():
+            for i in range(images):
+                cot_far(i).wait()
+                gate = scal_ref[i, 5].astype(F32) * KEEP_SCALE
+                live = row_valid(scal_ref, i, rows, half, 0)
+                d_mlp = (jnp.where(live, cot[i].astype(F32), 0.0) * gate).astype(BF16)
+                right[i] = d_mlp
+                vec[11:12, :] += jnp.sum(d_mlp.astype(F32), axis=0, keepdims=True)
+
+        for i in range(images):
+            d_pre = (djoin[i, :, 2 * width :].astype(F32) * dot_nt(right[i], wbuf[2 + slot])).astype(BF16)
             djoin[i, :, width : 2 * width] = d_pre
             vec[pl.ds(7 + t, 1), :] += jnp.sum(d_pre.astype(F32), axis=0, keepdims=True)
-            acc[i] += dot_nn(hidden, wbuf[2 + slot])
             dn2[i] += dot_nt(d_pre, wbuf[slot])
 
         tile[...] = dot_tn(column(0), flat(right))
@@ -1018,10 +1069,9 @@
 
     wqkv_copy(1, 1).start()
     wqkv_copy(2, 3).start()
-    unit_in, att_in, rstd_in = fetch(unit_hbm, left), fetch(att_hbm, right), fetch(rstd_hbm, rstd_one)
+    unit_in, att_in = fetch(unit_hbm, left), fetch(att_hbm, right)
     start(FC2_B)
     start(FC1_B)
-    mid_in.wait()
     for i in range(images):
         gate = scal_ref[i, 5].astype(F32) * KEEP_SCALE
         final = mid[i] + gate * (acc[i] + rows_ref[4:5, :])
@@ -1034,7 +1084,7 @@
         lambda: (gsend, out_ref.at[pl.ds(x * images, images)]), lambda: side_send.at[images], lambda: side_recv.at[images], across
     )
 
-    wp_copy.wait()
+    wp_copy(2).wait()
     for i in range(images):
         live = row_valid(scal_ref, i, rows, half, 0)
         d_final = jnp.where(live, cot[i].astype(F32), 0.0)
@@ -1048,39 +1098,22 @@
         d_branch = (d_middle * gate).astype(BF16)
         datt[i] = d_branch
         vec[4:5, :] += jnp.sum(d_branch.astype(F32), axis=0, keepdims=True)
-    parcels[FC2_A].move(1)
+    at_point("norm")
     unit_in.wait()
     att_in.wait()
-    rstd_in.wait()
     tile[...] = dot_tn(flat(right), flat(datt))
     put_folds(send_b.at[0], keep_b.at[2], 1)
-    step_one(FC1_B)
+    at_point("proj")
     for i in range(images):
         datt[i] = dot_nt(datt[i], wbuf[2]).astype(BF16)
-    step_one(FC2_B)
-
-    low_lane = lax.broadcasted_iota(jnp.int32, (rows, 128), 1) < HEAD_DIM
-    sides = (low_lane, jnp.logical_not(low_lane))
-    cuts = lambda pair: [slice(k * width + 128 * pair, k * width + 128 * pair + 128) for k in range(3)]
+    at_point("back")
+
     total_pairs = images * pairs
 
     def next_probs(index, slot):
         @pl.when(index + SLOTS < 2 * total_pairs)
         def _():
             probs_copy((index + SLOTS) % total_pairs, slot).start()
-
-    def pump(plan, i, pair):
-        for (image, at), job in plan.items():
-            if at == pair:
-
-                @pl.when(i == image)
-                def _():
-                    job()
-
-    early_plan = {
-        (0, 4): lambda: parcels[FC1_A].move(1),
-        (2, 3): lambda: parcels[FC2_A].move(2),
-    }
 
     @pl.loop(0, images)
     def _(i):
@@ -1093,21 +1126,12 @@
             dv = dot_nn(probs[slot, 0], jnp.where(sides[0], a2, 0)) + dot_nn(probs[slot, 1], jnp.where(sides[1], a2, 0))
             djoin[i, :, v_cut] = dv.astype(BF16)
             next_probs(index, slot)
-            pump(early_plan, i, pair)
+            pump(plan_of("b"), i, pair)
         vec[3:4, :] += jnp.sum(djoin[i, :, 2 * width :].astype(F32), axis=0, keepdims=True)
 
     tile[...] = dot_tn(flat(left), column(2))
     put_folds(send_b.at[0], keep_b.at[2], 0)
     start(VAL_PROJ)
-
-    plan = {
-        (0, 5): lambda: parcels[FC1_B].move(1),
-        (1, 0): lambda: step_one(VAL_PROJ),
-        (1, 3): lambda: parcels[FC2_A].move(3),
-        (1, 4): lambda: parcels[FC1_A].move(2),
-        (2, 2): lambda: parcels[FC2_B].move(1),
-        (2, 3): lambda: parcels[FC1_B].move(2),
-    }
 
     @pl.loop(0, images)
     def _(i):
@@ -1130,7 +1154,7 @@
             djoin[i, :, q_cut] = (dq * HEAD_DIM**-0.5).astype(BF16)
             djoin[i, :, k_cut] = dk.astype(BF16)
             next_probs(index, slot)
-            pump(plan, i, pair)
+            pump(plan_of("c"), i, pair)
 
         @pl.when(i + 2 < images)
         def _():
@@ -1143,6 +1167,7 @@
         tile[...] = dot_tn(flat(left), column(t))
         put_folds(send_c.at[t], keep_c.at[t], 0)
         start(k)
+    at_point("key")
     wqkv_copy(0, 0).wait()
     wqkv_copy(1, 1).wait()
     wqkv_copy(2, 3).wait()
@@ -1163,15 +1188,6 @@
         trade.wait()
         vec[...] += vget[k]
 
-    def write_folds(total, ref, tile_at):
-        for t in range(total.shape[1] // side_cols):
-            for h in range(2):
-                at = (tile_at + t) * width + h * side_cols
-                ref[:, at : at + side_cols] = total[h * unit : h * unit + unit, t * side_cols : t * side_cols + side_cols]
-
-    def write_fc2(total):
-        fc2_ref[...] = total
-
     swaps = []
 
     def swap_out(i):
@@ -1179,61 +1195,37 @@
             Far(lambda: (gsend.at[i], grecv.at[i]), lambda: side_send.at[i], lambda: side_recv.at[i], across)
         )
 
-    trade = exchange(0)
-    input_grad(0)
-    swap_out(0)
-    settle(0, trade)
-    trade = exchange(1)
-    parcels[VAL_PROJ].move(1)
-    step_one(QUERY)
-    step_one(KEY)
-    input_grad(1)
-    swap_out(1)
-    settle(1, trade)
-    trade = exchange(2)
-    parcels[QUERY].move(1)
-    parcels[KEY].move(1)
-    input_grad(2)
-    swap_out(2)
-    settle(2, trade)
-    trade = exchange(3)
+    for i in range(images):
+        trade = exchange(i)
+        input_grad(i)
+        swap_out(i)
+        settle(i, trade)
+        if i + 1 < images:
+            at_point("input%d" % i)
     grad_own = pltpu.make_async_copy(acc.at[:, pl.ds(0, half)], grad_ref, out_sem.at[1])
     grad_own.start()
-    parcels[KEY].move(2)
-    parcels[FC1_B].move(3)
-    parcels[FC2_B].move(2)
+    trade = exchange(3)
+    at_point("input2")
     settle(3, trade)
     trade = exchange(4)
-    parcels[FC2_A].finish(write_fc2)
-    parcels[FC1_A].move(3)
-    parcels[QUERY].move(2)
-    parcels[VAL_PROJ].move(2)
+    at_point("end0")
     settle(4, trade)
     vec_ref[...] = vec[...]
-    parcels[FC2_B].move(3)
-    write_folds(parcels[FC1_B].gather(4), fc1_ref, 2)
-    parcels[KEY].move(3)
-    write_folds(parcels[FC1_A].gather(4), fc1_ref, 0)
-    parcels[QUERY].move(3)
-    parcels[VAL_PROJ].move(3)
-    write_folds(parcels[KEY].gather(4), qkvg_ref, 1)
-    parcels[FC2_B].finish(write_fc2)
-    write_folds(parcels[QUERY].gather(4), qkvg_ref, 0)
+    at_point("end1")
     for copy in swaps:
         copy.wait()
     grad_oth = pltpu.make_async_copy(grecv, back_ref, out_sem.at[2])
     grad_oth.start()
-    total = parcels[VAL_PROJ].gather(4)
-    write_folds(total[:, :side_cols], qkvg_ref, 2)
-    write_folds(total[:, side_cols:], projg_ref, 0)
     out_own.wait()
     grad_own.wait()
     grad_oth.wait()
 
 
-def rest(facts, cotangent, cot_oth, n2, middle, qkv, probs, unit_one, rstd_one, attended, rows_in, w):
-    images, half, width = cot_oth.shape
+def rest(facts, patches, cotangent, vectors, w):
+    all_images, half, width = patches.shape
+    images = all_images // 2
     rows = 2 * half
+    heads = width // HEAD_DIM
     hidden_width = w["fc1_weight"].shape[1]
     r, c = 2 * (width // GROUP), width
     fc2_rows = hidden_width // GROUP
@@ -1252,8 +1244,8 @@
     folds_of = lambda count, cols: pltpu.VMEM((count, 2, 2, 2, 2, r, cols), BF16)
     return pl.pallas_call(
         rest_kernel,
-        in_specs=[smem] * 4 + [hbm] * 13 + [vmem],
-        out_specs=[vmem] * 5 + [hbm] * 3,
+        in_specs=[smem] * 4 + [hbm] * 6 + [vmem] * 8,
+        out_specs=[vmem] * 5 + [hbm] * 7,
         out_shape=[
             jax.ShapeDtypeStruct((fc2_rows, width), F32),
             jax.ShapeDtypeStruct((r // 2, hidden_width), F32),
@@ -1263,9 +1255,13 @@
             jax.ShapeDtypeStruct((2 * images, half, width), BF16),
             jax.ShapeDtypeStruct((images, half, width), F32),
             jax.ShapeDtypeStruct((images, half, width), BF16),
+            jax.ShapeDtypeStruct((images, rows, width), BF16),
+            jax.ShapeDtypeStruct((images, rows, 3 * width), BF16),
+            jax.ShapeDtypeStruct((images, heads, rows, rows), BF16),
+            jax.ShapeDtypeStruct((images, rows, width), BF16),
         ],
         scratch_shapes=[
-            whole(BF16), pltpu.VMEM((images, rows, 1), F32), whole(F32), whole(F32), whole(F32), whole(BF16), whole(BF16),
+            whole(BF16), pltpu.VMEM((images, rows, 1), F32), pltpu.VMEM((16, width), F32), whole(F32), whole(F32), whole(F32), whole(BF16), whole(BF16),
             pltpu.VMEM((4, width, width), BF16),
             pltpu.VMEM((2, rows, 3 * width), BF16),
             pltpu.VMEM((SLOTS, 2, rows, rows), BF16),
@@ -1279,13 +1275,13 @@
             folds_of(3, c), folds_of(2, c), folds_of(2, c),
             folds_of(2, c // 2), folds_of(2, c // 2), folds_of(2, c // 2),
             *level_bufs,
-            dma((8,)), dma((SLOTS,)), dma((2,)), dma((4,)), dma((PARTS, 5)), dma((PARTS, 5)), dma((images + 1,)),
+            dma((4,)), dma((SLOTS,)), dma((2,)), dma((4,)), dma((5 * images,)), dma((2 * images,)), dma((2 * images,)),
+            dma((PARTS, 5)), dma((PARTS, 5)), dma((images + 1,)),
             dma((images + 1,)), dma((5,)), dma((5,)), dma((3,)), pltpu.SemaphoreType.REGULAR((2,)),
         ],
         compiler_params=pltpu.CompilerParams(collective_id=0, has_side_effects=True, vmem_limit_bytes=64 * MIB),
         name="rest",
-    )(*facts, cotangent, cot_oth, n2, middle, qkv, probs, w["fc1_weight"], w["fc2_weight"], w["proj_weight"],
-      w["qkv_weight"], unit_one, rstd_one, attended, rows_in)
+    )(*facts, patches, cotangent, w["fc1_weight"], w["fc2_weight"], w["proj_weight"], w["qkv_weight"], *vectors)
 
 
 def spread(value):
@@ -1352,17 +1348,13 @@
     unit2 = fc2_weight.shape[0] // GROUP
     if owners == GROUP:
         merge = lambda v: v.reshape(all_images, half, width)
-        facts = (grid_shape, split_rows, owner_shard, drop_masks)
-        unit_one, rstd_one, qkv, probs, attended, middle, n2, rows_in, c_oth = opening(
+        facts = (grid_shape.T, split_rows, owner_shard, drop_masks.T)
+        fc2_part, fc1_part, u_part, proj_part, sums, out_part, grad_own, grad_back, *_ = rest(
             facts, merge(patches), merge(cotangent),
-            (ln1_gain, ln1_bias, qv_bias, proj_bias, ln2_gain, ln2_bias, fc1_bias, fc2_bias, qkv_weight, proj_weight),
-        )
-        fc2_part, fc1_part, u_part, proj_part, sums, out_part, grad_own, grad_back = rest(
-            facts, merge(cotangent), c_oth, n2, middle, qkv, probs, unit_one, rstd_one, attended, rows_in, w
+            (ln1_gain, ln1_bias, qv_bias, proj_bias, ln2_gain, ln2_bias, fc1_bias, fc2_bias), w,
         )
         outs = emit(
-            fc2_part, fc1_part, u_part, proj_part, sums, rows_in, qkv_weight,
-            grad_own, grad_back, out_part,
+            fc2_part, fc1_part, u_part, proj_part, sums, ln1_gain, ln1_bias, qkv_weight, grad_own, grad_back, out_part
         )
         layer_out, patches_grad = (v.reshape(all_images, 1, half, width) for v in outs[:2])
         return (layer_out, patches_grad, *outs[2:])

time: 176 us -> 163 us (0.926); the launches traced: 173 us -> 162 us
  Pallas kernels: 170 us -> 161 us
  local copies, waits for them, and re-layouts: 2.7 us -> 0 us
    pallas_call x2 -> x1, Pallas kernels: 164 us -> 156 us  [rest(): pl.pallas_call(rest_kernel, in_specs=[smem] * 4 + [hbm] * 6 + [vmem] * 8,...]
    unnamed x2 -> x0, local copies, waits for them, and re-layouts: 2.7 us -> none
where the time goes in v1:
time: 163 us; the launch traced here: 162 us
  Pallas kernels  161 us (99%)
    pallas_call x1, Pallas kernels, rest(): pl.pallas_call(rest_kernel, in_specs=[smem] * 4 + [hbm] * 6 + [vmem] * 8,...  156 us
    pallas_call x1, Pallas kernels, emit(): pl.pallas_call(emit_kernel, grid=(1,), in_specs=[whole(v) for v in (fc2,...  5.54 us

profile of v1, /device:TPU:0, one launch (start us, length us, event | category | flops | bytes accessed | tf_op | source)
XLA Modules:
  0.0 162.3 jit_solution(72636614890655111)
XLA Ops:
  0.7 155.9 %rest.1 = (f32[96,768]{1,0:T(8,128)}, f32[24,3072]{1,0:T(8,128)}, f32[24,2304]{1,0:T(8,128)}, f32[24,768]{1,0:T(8,128)}, f32[16,768]{1,0:T(8,128)}, /*index=5*/b...) custom-call(s32[2,6]{1,0:T(2,128)} %bitcast.12, ...), custom_call_target="tpu_custom_call" | custom-call | tf_op jit(solution)/shard_map/rest/pallas_call | solution.py:1245
  156.5 5.5 %emit.1 = (bf16[6,160,768]{2,1,0:T(8,128)(2,1)}, f32[6,160,768]{2,1,0:T(8,128)}, f32[24]{0:T(128)}, f32[24]{0:T(128)}, f32[24,2304]{1,0:T(8,128)}, /*index=5*/f3...) custom-call(f32[96,768]{1,0:T(8,128)} %get-tuple-element.36.fc2_ref,, ...), custom_call_target="tpu_custom_call" | custom-call | tf_op jit(solution)/shard_map/emit/pallas_call | solution.py:565

commit v2 on v1

--- a/solution.py
+++ b/solution.py
@@ -639,10 +639,9 @@
                 i = i // 2
             inner = tuple(at[n] for n in left)
             spot = tuple(at[n] if n in at else self.place[n][0] for n in self.names)
-            total = self.keep()[spot].astype(F32) + arrived[inner].astype(F32)
             if step == len(self.order):
-                return total
-            self.keep()[spot] = total.astype(BF16)
+                return self.keep()[spot].astype(F32) + arrived[inner].astype(F32)
+            self.keep()[spot] = self.keep()[spot] + arrived[inner]
 
         if not left:
             return one(0)

time: 163 us -> 162 us (level)
  no operation moved by 1% of the time
where the time goes in v2:
time: 162 us; the launch traced here: 161 us
  Pallas kernels  160 us (99%)
    pallas_call x1, Pallas kernels, rest(): pl.pallas_call(rest_kernel, in_specs=[smem] * 4 + [hbm] * 6 + [vmem] * 8,...  155 us
    pallas_call x1, Pallas kernels, emit(): pl.pallas_call(emit_kernel, grid=(1,), in_specs=[whole(v) for v in (fc2,...  5.54 us

profile of v2, /device:TPU:0, one launch (start us, length us, event | category | flops | bytes accessed | tf_op | source)
XLA Modules:
  0.0 161.2 jit_solution(6579359688163365157)
XLA Ops:
  0.7 154.8 %rest.1 = (f32[96,768]{1,0:T(8,128)}, f32[24,3072]{1,0:T(8,128)}, f32[24,2304]{1,0:T(8,128)}, f32[24,768]{1,0:T(8,128)}, f32[16,768]{1,0:T(8,128)}, /*index=5*/b...) custom-call(s32[2,6]{1,0:T(2,128)} %bitcast.12, ...), custom_call_target="tpu_custom_call" | custom-call | tf_op jit(solution)/shard_map/rest/pallas_call | solution.py:1244
  155.4 5.5 %emit.1 = (bf16[6,160,768]{2,1,0:T(8,128)(2,1)}, f32[6,160,768]{2,1,0:T(8,128)}, f32[24]{0:T(128)}, f32[24]{0:T(128)}, f32[24,2304]{1,0:T(8,128)}, /*index=5*/f3...) custom-call(f32[96,768]{1,0:T(8,128)} %get-tuple-element.36.fc2_ref,, ...), custom_call_target="tpu_custom_call" | custom-call | tf_op jit(solution)/shard_map/emit/pallas_call | solution.py:565
